TPU v7x, 1024 devices: a whole 8x8x8 slice. The times are simulated.
1024 devices in a mesh: seq: 64 (over z, y), heads: 8 (over x), dp: 2 (over core).
Axes of the slice: x: 8, y: 8, z: 8, core: 2. Of those that a mesh axis runs over, the one named last changes fastest.
Arguments:
- queries: bfloat16 [16384, 4096], P(('dp', 'seq'), 'heads'), parts along dimension 0, may hold values from -7 to 7
- keys: bfloat16 [16384, 4096], P(('dp', 'seq'), 'heads'), parts along dimension 0, may hold values from -7 to 7
- values: bfloat16 [16384, 4096], P(('dp', 'seq'), 'heads'), parts along dimension 0, may hold values from -6 to 6
- out_grad: bfloat16 [16384, 4096], P(('dp', 'seq'), 'heads'), parts along dimension 0, may hold values from -6 to 6
- random_blocks: int32 [64, 3, 128], P(('dp', 'heads')), parts along dimension 0, may hold values from 0 to 127, as said below
- global_blocks: int32 [4], P('dp'), parts along dimension 0, may hold values from 0 to 127
Outputs:
- attended: bfloat16 [16384, 4096], P(('dp', 'seq'), 'heads'), parts along dimension 0
- query_grad: bfloat16 [16384, 4096], P(('dp', 'seq'), 'heads'), parts along dimension 0
- key_grad: bfloat16 [16384, 4096], P(('dp', 'seq'), 'heads'), parts along dimension 0
- value_grad: bfloat16 [16384, 4096], P(('dp', 'seq'), 'heads'), parts along dimension 0
There are 2 independent parts, one for each index of `dp`. A program takes and returns all parts, laid end to end along the dimension named above; each array names one. Nothing has to cross between parts.
Inputs may be any that keep to these rules, and one draw needn't show every extreme that they name: `random_blocks`: entries are key block numbers. Among the entries of the 2 query blocks of one index of seq and the 4 heads of one index of heads, at most 1 name blocks of the same index of seq (block // 2), and some index of seq is named exactly 1 times.
All inputs are finite; a program needn't handle non-finite values.
Results may differ from a plain program's by a relative error of at most 0.024.
Values may be sent and summed in bfloat16 or wider, within the bound.
A program may use at most 32 MiB of HBM per device.

v0:
```python
import jax
import jax.numpy as jnp
from jax import lax
from jax.sharding import PartitionSpec as P


def from_root(value, axis, source):
    kept = jnp.where(lax.axis_index(axis) == source, value, 0).astype(value.dtype)
    return lax.psum(kept, axis)


def with_halo(cells, sides, width):
    for axis, dim in sides:
        count = lax.axis_size(axis)
        ends = count - 1
        head = lax.slice_in_dim(cells, 0, width, axis=dim)
        tail = lax.slice_in_dim(cells, cells.shape[dim] - width, cells.shape[dim], axis=dim)
        cells = jnp.concatenate(
            [
                lax.ppermute(tail, axis, [(i, (i + 1) % count) for i in range(ends)]),
                cells,
                lax.ppermute(head, axis, [((i + 1) % count, i) for i in range(ends)]),
            ],
            axis=dim,
        )
    return cells


def fetch_global(kv_blocks, spot, owner):
    piece = lax.dynamic_index_in_dim(kv_blocks, spot, 1, keepdims=False)
    return from_root(piece, "seq", owner)


def body(queries, keys, values, out_grad, random_blocks, global_blocks):
    row_count, local_width = queries.shape
    seq_count = lax.axis_size("seq")
    self_index = lax.axis_index("seq")
    head_count, rand_count, total_blocks = random_blocks.shape
    block_table = random_blocks.transpose(2, 0, 1)
    block_count = total_blocks // seq_count
    block_rows = row_count // block_count
    head_size = local_width // head_count
    glob_count = global_blocks.shape[0]
    score_scale = head_size ** (-0.5)
    item_count = block_count * head_count * rand_count
    capacity = (item_count + seq_count - 1) // seq_count
    slot_total = seq_count * capacity
    slot_count = 3 + rand_count + glob_count
    key_rows = slot_count * block_rows
    query_blocks = queries.reshape(block_count, block_rows, head_count, head_size)
    grad_blocks = out_grad.reshape(block_count, block_rows, head_count, head_size)
    stacked_kv = jnp.stack([keys, values])
    kv_blocks = stacked_kv.reshape(2, block_count, block_rows, head_count, head_size)
    extended = with_halo(stacked_kv, (("seq", 1),), block_rows)
    ext_blocks = extended.reshape(2, block_count + 2, block_rows, head_count, head_size)
    window = jnp.stack(
        [
            ext_blocks[:, 0:block_count],
            ext_blocks[:, 1 : block_count + 1],
            ext_blocks[:, 2 : block_count + 2],
        ],
        2,
    )
    owners = global_blocks // block_count
    spots = global_blocks % block_count
    glob_kv = jnp.stack(
        [fetch_global(kv_blocks, spots[number], owners[number]) for number in range(glob_count)], 1
    )
    glob_kv = jnp.broadcast_to(
        glob_kv[:, None], (2, block_count, glob_count, block_rows, head_count, head_size)
    )
    flat_lists = block_table.reshape(seq_count, item_count)
    item_ids = jnp.arange(item_count, dtype=jnp.int32)
    item_head = item_ids // rand_count % head_count
    mine = flat_lists // block_count == self_index
    ranks = jnp.cumsum(mine.astype(jnp.int32), 1) - 1
    slot_ids = jnp.arange(capacity, dtype=jnp.int32)
    chosen = (mine[:, None, :] & (ranks[:, None, :] == slot_ids[None, :, None])).astype(jnp.int32)
    slot_used = (jnp.sum(chosen, -1) > 0).reshape(slot_total)
    send_block = jnp.sum(chosen * (flat_lists % block_count)[:, None, :], -1).reshape(slot_total)
    send_head = jnp.sum(chosen * item_head[None, None, :], -1).reshape(slot_total)
    block_range = jnp.arange(block_count, dtype=jnp.int32)
    head_range = jnp.arange(head_count, dtype=jnp.int32)
    selector = (
        slot_used[:, None, None]
        & (send_block[:, None, None] == block_range[None, :, None])
        & (send_head[:, None, None] == head_range[None, None, :])
    ).astype(jnp.bfloat16)
    outgoing = jnp.einsum(
        "sbh,cbrhd->scrd", selector, kv_blocks, preferred_element_type=jnp.float32
    ).astype(jnp.bfloat16)
    incoming = lax.all_to_all(outgoing, "seq", split_axis=0, concat_axis=0, tiled=True)
    wanted = lax.dynamic_index_in_dim(flat_lists, self_index, 0, keepdims=False)
    source = wanted // block_count
    earlier = (source[:, None] == source[None, :]) & (item_ids[None, :] < item_ids[:, None])
    position = source * capacity + jnp.sum(earlier.astype(jnp.int32), 1)
    placing = (position[:, None] == jnp.arange(slot_total, dtype=jnp.int32)[None, :]).astype(
        jnp.bfloat16
    )
    fetched = jnp.einsum(
        "ps,scrd->pcrd", placing, incoming, preferred_element_type=jnp.float32
    ).astype(jnp.bfloat16)
    fetched = fetched.reshape(
        block_count, head_count, rand_count, 2, block_rows, head_size
    ).transpose(3, 0, 2, 4, 1, 5)
    all_kv = jnp.concatenate([window, fetched, glob_kv], 2).reshape(
        2, block_count, key_rows, head_count, head_size
    )
    key_all = all_kv[0]
    value_all = all_kv[1]
    block_ids = self_index * block_count + block_range
    always = jnp.ones((block_count,), dtype=bool)
    slot_valid = jnp.stack(
        [block_ids >= 1, always, block_ids <= total_blocks - 2]
        + [always] * (rand_count + glob_count),
        1,
    )
    row_valid = jnp.repeat(slot_valid, block_rows, axis=1)
    scores = (
        jnp.einsum("bqhd,bkhd->bhqk", query_blocks, key_all, preferred_element_type=jnp.float32)
        * score_scale
    )
    scores = jnp.where(row_valid[:, None, None, :], scores, -jnp.inf)
    row_max = jnp.max(scores, -1, keepdims=True)
    log_total = row_max + jnp.log(jnp.sum(jnp.exp(scores - row_max), -1, keepdims=True))
    probs = jnp.exp(scores - log_total)
    probs_low = probs.astype(jnp.bfloat16)
    attended = jnp.einsum(
        "bhqk,bkhd->bqhd", probs_low, value_all, preferred_element_type=jnp.float32
    ).astype(jnp.bfloat16)
    delta_rows = jnp.sum(grad_blocks.astype(jnp.float32) * attended.astype(jnp.float32), -1)
    delta_rows = delta_rows.transpose(0, 2, 1)[..., None]
    prob_grad = jnp.einsum(
        "bqhd,bkhd->bhqk", grad_blocks, value_all, preferred_element_type=jnp.float32
    )
    score_grad = (score_scale * probs * (prob_grad - delta_rows)).astype(jnp.bfloat16)
    query_grad = jnp.einsum(
        "bhqk,bkhd->bqhd", score_grad, key_all, preferred_element_type=jnp.float32
    ).astype(jnp.bfloat16)
    key_terms = jnp.einsum(
        "bhqk,bqhd->bkhd", score_grad, query_blocks, preferred_element_type=jnp.float32
    )
    value_terms = jnp.einsum(
        "bhqk,bqhd->bkhd", probs_low, grad_blocks, preferred_element_type=jnp.float32
    )
    terms = jnp.stack([key_terms, value_terms]).reshape(
        2, block_count, slot_count, block_rows, head_count, head_size
    )
    random_back = terms[:, :, 3 : 3 + rand_count].astype(jnp.bfloat16)
    placement = placing.reshape(block_count, head_count, rand_count, slot_total).transpose(
        3, 0, 2, 1
    )
    parcel = jnp.einsum(
        "sbrh,cbrjhd->scjd", placement, random_back, preferred_element_type=jnp.float32
    ).astype(jnp.bfloat16)
    returned = lax.all_to_all(parcel, "seq", split_axis=0, concat_axis=0, tiled=True)
    accum = jnp.einsum("sbh,scrd->cbrhd", selector, returned, preferred_element_type=jnp.float32)
    left_terms = terms[:, :, 0]
    right_terms = terms[:, :, 2]
    zero_block = jnp.zeros((2, 1, block_rows, head_count, head_size), jnp.float32)
    accum = accum + terms[:, :, 1]
    accum = accum + jnp.concatenate([left_terms[:, 1:], zero_block], 1)
    accum = accum + jnp.concatenate([zero_block, right_terms[:, : block_count - 1]], 1)
    rims = jnp.concatenate([left_terms[:, 0], right_terms[:, block_count - 1]], 1).reshape(
        2, 2 * block_rows, local_width
    )
    rim_back = with_halo(rims.astype(jnp.bfloat16), (("seq", 1),), block_rows).astype(rims.dtype)
    from_left = rim_back[:, 0:block_rows].reshape(2, block_rows, head_count, head_size)
    from_right = rim_back[:, 3 * block_rows : 4 * block_rows].reshape(
        2, block_rows, head_count, head_size
    )
    accum = accum.at[:, 0].add(from_left)
    accum = accum.at[:, block_count - 1].add(from_right)
    glob_terms = jnp.sum(terms[:, :, 3 + rand_count :], 1)
    glob_total = lax.psum(glob_terms, "seq")
    for number in range(glob_count):
        share = glob_total[:, number] * (self_index == owners[number]).astype(jnp.float32)
        current = lax.dynamic_index_in_dim(accum, spots[number], 1, keepdims=True)
        accum = lax.dynamic_update_index_in_dim(accum, current + share[:, None], spots[number], 1)
    key_grad = accum[0].reshape(row_count, local_width).astype(jnp.bfloat16)
    value_grad = accum[1].reshape(row_count, local_width).astype(jnp.bfloat16)
    return (
        attended.reshape(row_count, local_width),
        query_grad.reshape(row_count, local_width),
        key_grad,
        value_grad,
    )


def solution(mesh):
    in_specs = (
        P(("dp", "seq"), "heads"),
        P(("dp", "seq"), "heads"),
        P(("dp", "seq"), "heads"),
        P(("dp", "seq"), "heads"),
        P(("dp", "heads"), None, None),
        P("dp"),
    )
    out_specs = (
        P(("dp", "seq"), "heads"),
        P(("dp", "seq"), "heads"),
        P(("dp", "seq"), "heads"),
        P(("dp", "seq"), "heads"),
    )
    return jax.shard_map(body, mesh=mesh, in_specs=in_specs, out_specs=out_specs, check_vma=False)
```

profile of v0, /device:TPU:14, one launch (start us, length us, event | category | flops | bytes accessed | tf_op | source)
XLA Modules:
  0.0 463.0 jit_solution(8655977238019489384)
XLA Ops:
  7.2 0.9 copy.126
  8.4 0.9 stack.53
  9.4 0.9 stack.54
  10.9 0.8 bitcast_convert_fusion
  11.7 2.7 copy.130
  14.4 23.6 %all-to-all-start = ((bf16[64,2,64,128]{3,2,1,0:T(8,128)(2,1)}), bf16[64,2,64,128]{3,2,1,0:T(8,128)(2,1)S(1)}, u32[]{:S(2)}, u32[]{:S(2)}) async-start(bf16[64,2,64,128]{3,2,1,0:T(8,128)(2,1)} %copy.130), calls=%async_computation | async-start | bytes 4194304 | tf_op jit(solution)/shard_map/all_to_all | solution.py:92
  38.1 1.3 collective-permute-start.1
  39.4 5.2 %collective-permute-start = (bf16[2,64,512]{2,1,0:T(8,128)(2,1)S(1)}, bf16[2,64,512]{2,1,0:T(8,128)(2,1)}, u32[]{:S(2)}, u32[]{:S(2)}) collective-permute-start(bf16[2,64,512]{2,1,0:T(8,128)(2,1)S(1)} %get-tuple-element.46), channel_id=1, source_target_pairs={{0,16},{16,32},{32,48},{48,64},{64,80},{80,96},{96,112},{112,128},... | collective-permute-start | bytes 393224 | tf_op jit(solution)/shard_map/ppermute | solution.py:20
  52.2 35.6 %collective-permute-done.1 = bf16[2,64,512]{2,1,0:T(8,128)(2,1)} collective-permute-done((bf16[2,64,512]{2,1,0:T(8,128)(2,1)S(1)}, bf16[2,64,512]{2,1,0:T(8,128)(2,1)}, u32[]{:S(2)}, u32[]{:S(2)}) %collective-permute-start.1) | collective-permute-done | bytes 131104 | tf_op jit(solution)/shard_map/ppermute | solution.py:22
  87.8 1.0 pad_maximum_fusion
  91.6 142.6 %all-reduce.8.cloned.1.call-done = (bf16[2,1,64,4,128]{4,3,1,2,0:T(4,128)(2,1)}, bf16[2,1,64,4,128]{4,3,1,2,0:T(4,128)(2,1)}) async-done(((bf16[2,1,64,4,128]{4,3,1,2,0:T(4,128)(2,1)}, bf16[2,1,64,4,128]{4,3,1,2,0:T(4,128)(2,1)}), (bf16[2,1,64,4,128]{4,3,1,2,0:T(4,128)(2,1)}, bf16[2,1,64,4,128]{4,3,1,2,0:T(4,128)(2,1)})) %all-reduce.8.cloned.1.call-update) | async-done | bytes 262160 | tf_op jit(solution)/shard_map/psum | solution.py:9
  234.2 1.2 pad_maximum_fusion.1
  235.4 1.3 fusion.4
  236.9 1.1 constant_dynamic-update-slice_fusion.2
  238.0 1.0 broadcast_dynamic-update-slice_fusion
  239.0 1.8 fusion.74
  243.8 1.4 copy_dynamic-update-slice_fusion.1
  245.2 1.5 copy_dynamic-update-slice_fusion
  246.7 1.0 bitcast_convert_fusion.1
  247.7 1.0 copy-done
  248.6 2.7 copy.147
  251.3 8.3 %all-to-all-start.1 = ((bf16[64,2,64,128]{3,2,1,0:T(8,128)(2,1)}), bf16[64,2,64,128]{3,2,1,0:T(8,128)(2,1)}, u32[]{:S(2)}, u32[]{:S(2)}) async-start(bf16[64,2,64,128]{3,2,1,0:T(8,128)(2,1)} %copy.147), calls=%async_computation.1 | async-start | bytes 4194304 | tf_op jit(solution)/shard_map/all_to_all | solution.py:156
  259.9 1.4 slice_bitcast_fusion.1
  263.5 1.3 collective-permute-start.3
  264.8 4.6 collective-permute-start.2
  269.4 2.4 slice_reduce_fusion
  271.9 33.0 %collective-permute-done.3 = bf16[2,64,512]{2,1,0:T(8,128)(2,1)S(1)} collective-permute-done((bf16[2,64,512]{2,1,0:T(8,128)(2,1)S(1)}, bf16[2,64,512]{2,1,0:T(8,128)(2,1)S(1)}, u32[]{:S(2)}, u32[]{:S(2)}) %collective-permute-start.3) | collective-permute-done | bytes 131104 | tf_op jit(solution)/shard_map/ppermute | solution.py:22
  305.1 4.9 %all-to-all-done.1 = bf16[64,2,64,128]{3,2,1,0:T(8,128)(2,1)} async-done(((bf16[64,2,64,128]{3,2,1,0:T(8,128)(2,1)}), bf16[64,2,64,128]{3,2,1,0:T(8,128)(2,1)}, u32[]{:S(2)}, u32[]{:S(2)}) %all-to-all-start.1) | async-done | bytes 2097184 | tf_op jit(solution)/shard_map/all_to_all | solution.py:156
  310.0 3.0 fusion.21
  313.2 139.1 %all-reduce.6.cloned.1.call-done = f32[2,2,64,4,128]{4,3,1,2,0:T(4,128)} async-done(((f32[2,2,64,4,128]{4,3,1,2,0:T(4,128)}), f32[2,2,64,4,128]{4,3,1,2,0:T(4,128)}) %all-reduce.6.cloned.1.call-update) | async-done | bytes 524304 | tf_op jit(solution)/shard_map/psum | solution.py:175
  452.3 1.1 fusion.30
  453.4 1.1 fusion.28
  (89 shorter events, 13.9 us)
Async XLA Ops:
  10.9 0.8 copy-start.5
  14.4 23.6 %copy-start.1 = (bf16[128,512]{1,0:T(8,128)(2,1)S(1)}, bf16[128,512]{1,0:T(8,128)(2,1)}, u32[]{:S(2)}) copy-start(bf16[128,512]{1,0:T(8,128)(2,1)} %param.11) | copy-start | bytes 393220
  14.4 23.6 %copy-start.2 = (bf16[128,512]{1,0:T(8,128)(2,1)S(1)}, bf16[128,512]{1,0:T(8,128)(2,1)}, u32[]{:S(2)}) copy-start(bf16[128,512]{1,0:T(8,128)(2,1)} %param.12) | copy-start | bytes 393220
  14.4 30.2 %copy-start.7 = (s32[2]{0:T(128)S(1)}, s32[2]{0:T(128)}, u32[]{:S(2)}) copy-start(s32[2]{0:T(128)} %param.15) | copy-start | bytes 28
  14.4 36.8 %copy-start.3 = (bf16[128,512]{1,0:T(8,128)(2,1)S(1)}, bf16[128,512]{1,0:T(8,128)(2,1)}, u32[]{:S(2)}) copy-start(bf16[128,512]{1,0:T(8,128)(2,1)} %param.13) | copy-start | bytes 393220
  14.4 36.9 %copy-start.4 = (bf16[128,512]{1,0:T(8,128)(2,1)S(1)}, bf16[128,512]{1,0:T(8,128)(2,1)}, u32[]{:S(2)}) copy-start(bf16[128,512]{1,0:T(8,128)(2,1)} %param.10) | copy-start | bytes 393220
  14.4 220.9 %all-to-all-start = ((bf16[64,2,64,128]{3,2,1,0:T(8,128)(2,1)}), bf16[64,2,64,128]{3,2,1,0:T(8,128)(2,1)S(1)}, u32[]{:S(2)}, u32[]{:S(2)}) async-start(bf16[64,2,64,128]{3,2,1,0:T(8,128)(2,1)} %copy.130), calls=%async_computation | async-start | bytes 4194304 | tf_op jit(solution)/shard_map/all_to_all | solution.py:92
  38.0 196.2 %all-reduce.8.cloned.1.call-start = ((), (), s32[]{:S(2)}) async-start(), calls=%async_computation.3 | async-start | bytes 524288 | tf_op jit(solution)/shard_map/psum | solution.py:9
  38.1 49.7 %collective-permute-start.1 = (bf16[2,64,512]{2,1,0:T(8,128)(2,1)S(1)}, bf16[2,64,512]{2,1,0:T(8,128)(2,1)}, u32[]{:S(2)}, u32[]{:S(2)}) collective-permute-start(bf16[2,64,512]{2,1,0:T(8,128)(2,1)S(1)} %get-tuple-element.47), channel_id=1, source_target_pairs={{16,0},{32,16},{48,32},{64,48},{80,64},{96,80},{112,96},{128,112},... | collective-permute-start | bytes 393224 | tf_op jit(solution)/shard_map/ppermute | solution.py:22
  39.4 48.4 %collective-permute-start = (bf16[2,64,512]{2,1,0:T(8,128)(2,1)S(1)}, bf16[2,64,512]{2,1,0:T(8,128)(2,1)}, u32[]{:S(2)}, u32[]{:S(2)}) collective-permute-start(bf16[2,64,512]{2,1,0:T(8,128)(2,1)S(1)} %get-tuple-element.46), channel_id=1, source_target_pairs={{0,16},{16,32},{32,48},{48,64},{64,80},{80,96},{96,112},{112,128},... | collective-permute-start | bytes 393224 | tf_op jit(solution)/shard_map/ppermute | solution.py:20
  246.7 1.9 copy-start
  251.3 58.7 %all-to-all-start.1 = ((bf16[64,2,64,128]{3,2,1,0:T(8,128)(2,1)}), bf16[64,2,64,128]{3,2,1,0:T(8,128)(2,1)}, u32[]{:S(2)}, u32[]{:S(2)}) async-start(bf16[64,2,64,128]{3,2,1,0:T(8,128)(2,1)} %copy.147), calls=%async_computation.1 | async-start | bytes 4194304 | tf_op jit(solution)/shard_map/all_to_all | solution.py:156
  259.6 192.8 %all-reduce.6.cloned.1.call-start = ((), (), s32[]{:S(2)}) async-start(), calls=%async_computation.2 | async-start | bytes 1048576 | tf_op jit(solution)/shard_map/psum | solution.py:175
  263.5 41.4 %collective-permute-start.3 = (bf16[2,64,512]{2,1,0:T(8,128)(2,1)S(1)}, bf16[2,64,512]{2,1,0:T(8,128)(2,1)S(1)}, u32[]{:S(2)}, u32[]{:S(2)}) collective-permute-start(bf16[2,64,512]{2,1,0:T(8,128)(2,1)S(1)} %concatenate.34), channel_id=1, source_target_pairs={{16,0},{32,16},{48,32},{64,48},{80,64},{96,80},{112,96},{128,112},... | collective-permute-start | bytes 393224 | tf_op jit(solution)/shard_map/ppermute | solution.py:22
  264.8 45.2 %copy-start.6 = (pred[64,2]{0,1:T(4,128)(4,1)S(1)}, pred[64,2]{0,1:T(4,128)(4,1)}, u32[]{:S(2)}) copy-start(pred[64,2]{0,1:T(4,128)(4,1)} %copy-done.5) | copy-start | bytes 388
  264.8 40.0 %collective-permute-start.2 = (bf16[2,64,512]{2,1,0:T(8,128)(2,1)S(1)}, bf16[2,64,512]{2,1,0:T(8,128)(2,1)S(1)}, u32[]{:S(2)}, u32[]{:S(2)}) collective-permute-start(bf16[2,64,512]{2,1,0:T(8,128)(2,1)S(1)} %concatenate.33), channel_id=1, source_target_pairs={{0,16},{16,32},{32,48},{48,64},{64,80},{80,96},{96,112},{112,128},... | collective-permute-start | bytes 393224 | tf_op jit(solution)/shard_map/ppermute | solution.py:20
Sparse Core Ops, SparseCore 0:
  51.3 182.7 all-reduce.7
  272.0 180.3 all-reduce.5
where the time goes:
time: 464 us; the launch traced here: 463 us
  waiting for transfers between devices  355 us (77%)
  starting transfers between devices  44.5 us (10%)
  local copies, waits for them, and re-layouts  25.5 us (5%)
  between operations  19.7 us (4%)
  matrix products  9.08 us (2%)
  other arithmetic  9.02 us (2%)
    psum x1, waiting for transfers between devices, from_root(): return lax.psum(kept, axis)  143 us
    psum x1, waiting for transfers between devices, body(): glob_total = lax.psum(glob_terms, 'seq')  139 us
    ppermute x2, waiting for transfers between devices, with_halo(): lax.ppermute(head, axis, [((i + 1) % count, i) for i in range(ends)])  68.6 us
    all_to_all x1, starting transfers between devices, body(): lax.all_to_all(outgoing, 'seq', split_axis=0, concat_axis=0, tiled=True)  23.6 us
    ppermute x2, starting transfers between devices, with_halo(): lax.ppermute(tail, axis, [(i, (i + 1) % count) for i in range(ends)])  9.76 us
  transfers between devices with their start and end apart: 8, of which 5 were waited for; matrix products, arithmetic and copies ran while one was open for 4% of the time, Pallas kernels for 0%

commit v1 on v0

v1 whole, which is shorter than its diff:
```python
import jax
import jax.numpy as jnp
from jax import lax
from jax.experimental import pallas as pl
from jax.experimental.pallas import tpu as pltpu
from jax.sharding import PartitionSpec as P

MESH = pl.DeviceIdType.MESH
BLK = 64
HD = 128
N = 8
HEADS = 4
NRAND = 3
NGLOB = 2
ITEMS = 2 * HEADS
CODE_K, CODE_V, INV, SRC, GLB = 0, 64, 128, 192, 216
SLOTS = N + 1
F32 = jnp.float32
BF16 = jnp.bfloat16
ROWS_T = (((1,), (1,)), ((), ()))
COLS_T = (((0,), (0,)), ((), ()))

AG = [(dr, s, c) for s in range(1, 5) for c in (0, 1) for dr in (1, -1) if s < 4 or (dr == 1) == (c == 0)]
FLOWS = [(1, 0, 4), (-1, 1, 4), (1, 1, 3), (-1, 0, 3)]
RS = [(f, s) for s in range(1, 5) for f in range(4) if s <= FLOWS[f][2]]


def kernel(
    tab, q, k, v, g,
    att, dq, dk, dv,
    agk, agv, wink, winv, sk, sv, rk, rv, gk, gv,
    ka, va, termk, termv, wk, wv, gak, gav, hsk, hsv, hrk, hrv,
    rsk, rsv, rrk, rrv, pk, pv, g2k, g2v, g3k, g3v,
    rsend, rrecv,
    lsem, ag_s, ag_r, h_s, h_r, b_s, b_r, gg_s, gg_r,
    hb_s, hb_r, rb_s, rb_r, g2_s, g2_r, g3_s, g3_r, rs_s, rs_r,
):
    me = lax.axis_index("seq")
    z = me // N
    y = me % N
    total = N * N

    def dev(axis, off):
        if axis == "y":
            return z * N + (y + off + N) % N
        return ((z + off + N) % N) * N + y

    pos = {"y": y, "z": z}

    def rc(src, dst, ss, rs, to):
        return pltpu.make_async_remote_copy(
            src_ref=src, dst_ref=dst, send_sem=ss, recv_sem=rs, device_id={"seq": to}, device_id_type=MESH
        )

    locals_ = []
    for i in range(ITEMS):
        part_of = (pl.ds(i // HEADS * BLK, BLK), pl.ds(i % HEADS * HD, HD))
        locals_.append(pltpu.make_async_copy(k.at[part_of], agk.at[y, i], lsem.at[i]))
        locals_.append(pltpu.make_async_copy(v.at[part_of], agv.at[z, i], lsem.at[ITEMS + i]))
    win_own = [
        pltpu.make_async_copy(k, wink.at[pl.ds(BLK, 2 * BLK)], lsem.at[2 * ITEMS]),
        pltpu.make_async_copy(v, winv.at[pl.ds(BLK, 2 * BLK)], lsem.at[2 * ITEMS + 1]),
    ]
    for c in locals_ + win_own:
        c.start()

    barrier = pltpu.get_barrier_semaphore()
    right_seq = (me + 1) % total
    left_seq = (me + total - 1) % total

    def greet(d, carry):
        pl.semaphore_signal(barrier, inc=1, device_id={"seq": dev("y", d)}, device_id_type=MESH)
        pl.semaphore_signal(barrier, inc=1, device_id={"seq": dev("z", d)}, device_id_type=MESH)
        return carry

    lax.fori_loop(1, N, greet, 0)
    pl.semaphore_signal(barrier, inc=1, device_id={"seq": right_seq}, device_id_type=MESH)
    pl.semaphore_signal(barrier, inc=1, device_id={"seq": left_seq}, device_id_type=MESH)
    for c in locals_:
        c.wait()
    pl.semaphore_wait(barrier, 2 * N)

    def ag_copy(arr, i):
        dr, s, c = AG[i]
        axis, buf = (("y", agk), ("z", agv))[arr]
        slot = (pos[axis] - dr * (s - 1) + N) % N
        rows = pl.ds(c * HEADS, HEADS)
        return rc(buf.at[slot, rows], buf.at[slot, rows], ag_s.at[arr, i], ag_r.at[arr, i], dev(axis, dr))

    def ag_wait(arr, i):
        dr, s, c = AG[i]
        axis, buf = (("y", agk), ("z", agv))[arr]
        slot = (pos[axis] - dr * s + N) % N
        rows = pl.ds(c * HEADS, HEADS)
        rc(buf.at[slot, rows], buf.at[slot, rows], ag_s.at[arr, i], ag_r.at[arr, i], dev(axis, dr)).wait_recv()

    index = {key: i for i, key in enumerate(AG)}
    for i, (dr, s, c) in enumerate(AG):
        if s == 1:
            for arr in (0, 1):
                ag_copy(arr, i).start()

    halo = [
        rc(k.at[pl.ds(BLK, BLK)], wink.at[pl.ds(0, BLK)], h_s.at[0], h_r.at[0], right_seq),
        rc(v.at[pl.ds(BLK, BLK)], winv.at[pl.ds(0, BLK)], h_s.at[1], h_r.at[1], right_seq),
        rc(k.at[pl.ds(0, BLK)], wink.at[pl.ds(3 * BLK, BLK)], h_s.at[2], h_r.at[2], left_seq),
        rc(v.at[pl.ds(0, BLK)], winv.at[pl.ds(3 * BLK, BLK)], h_s.at[3], h_r.at[3], left_seq),
    ]

    for i, (dr, s, c) in enumerate(AG):
        for arr in (0, 1):
            ag_wait(arr, i)
            nxt = index.get((dr, s + 1, c))
            if nxt is not None:
                ag_copy(arr, nxt).start()
        if i == 3:
            for c_ in halo:
                c_.start()
    for c in win_own:
        c.wait()

    def item(buf, slot, code):
        return buf[slot, code]

    gblk = [tab[GLB + i] for i in range(NGLOB)]

    def pick(idx):
        return jnp.where(idx // HEADS == 0, gblk[0], gblk[1])

    def far_first(j):
        return jnp.where(j % 2 == 1, N // 2 - (j + 1) // 2, N // 2 + j // 2)

    def fill(dst_k, dst_v, zd, yd):
        for s in range(N):
            dst_k[s] = item(agk, s, jnp.maximum(tab[CODE_K + zd * N + s], 0))
            dst_v[s] = item(agv, s, jnp.maximum(tab[CODE_V + yd * N + s], 0))
        blk = pick(y)
        dst_k[N] = item(agk, blk // 2 % N, blk % 2 * HEADS + y % HEADS)
        blk = pick(z)
        dst_v[N] = item(agv, blk // (2 * N), blk % 2 * HEADS + z % HEADS)

    def bundle(j, carry):
        d = far_first(j)
        zd = (z + d) % N
        yd = (y + d) % N
        fill(sk.at[j], sv.at[j], zd, yd)
        rc(sk.at[j], rk.at[z], b_s.at[0, j], b_r.at[0, j], zd * N + y).start()
        rc(sv.at[j], rv.at[y], b_s.at[1, j], b_r.at[1, j], z * N + yd).start()
        return carry

    lax.fori_loop(0, N - 1, bundle, 0)
    fill(rk.at[z], rv.at[y], z, y)

    def bundle_wait(j, carry):
        d = far_first(j)
        zs = (z + N - d) % N
        ys = (y + N - d) % N
        rc(sk.at[j], rk.at[zs], b_s.at[0, j], b_r.at[0, j], zs * N + y).wait_recv()
        rc(sv.at[j], rv.at[ys], b_s.at[1, j], b_r.at[1, j], z * N + ys).wait_recv()
        return carry

    lax.fori_loop(0, N - 1, bundle_wait, 0)

    gk[y] = rk[pick(y) // (2 * N), N]
    gv[z] = rv[pick(z) // 2 % N, N]

    def small(src_k, src_v, ss, rs, axis_k, axis_v):
        def start(j, carry):
            d = j + 1
            rc(src_k.at[pos[axis_k]], src_k.at[pos[axis_k]], ss.at[0, j], rs.at[0, j], dev(axis_k, d)).start()
            rc(src_v.at[pos[axis_v]], src_v.at[pos[axis_v]], ss.at[1, j], rs.at[1, j], dev(axis_v, d)).start()
            return carry

        lax.fori_loop(0, N - 1, start, 0)

    def small_wait(src_k, src_v, ss, rs, axis_k, axis_v):
        def wait(j, carry):
            d = N - 1 - j
            sl = (pos[axis_k] + d) % N
            rc(src_k.at[sl], src_k.at[sl], ss.at[0, j], rs.at[0, j], dev(axis_k, d)).wait_recv()
            sl = (pos[axis_v] + d) % N
            rc(src_v.at[sl], src_v.at[sl], ss.at[1, j], rs.at[1, j], dev(axis_v, d)).wait_recv()
            return carry

        lax.fori_loop(0, N - 1, wait, 0)

    small(gk, gv, gg_s, gg_r, "y", "z")
    for c_ in halo:
        c_.wait_recv()
    small_wait(gk, gv, gg_s, gg_r, "y", "z")

    scale = HD ** (-0.5)
    key_count = (3 + NRAND + NGLOB) * BLK

    def head(h, carry):
        cols = pl.ds(pl.multiple_of(h * HD, HD), HD)
        for b in range(2):
            rows = pl.ds(b * BLK, BLK)
            kb, vb = ka.at[b], va.at[b]
            kb[pl.ds(0, 3 * BLK)] = wink[pl.ds(b * BLK, 3 * BLK), cols]
            vb[pl.ds(0, 3 * BLK)] = winv[pl.ds(b * BLK, 3 * BLK), cols]
            for r in range(NRAND):
                src = tab[SRC + (h * NRAND + r) * 2 + b] // 2
                kb[pl.ds((3 + r) * BLK, BLK)] = rk[src // N, src % N]
                vb[pl.ds((3 + r) * BLK, BLK)] = rv[src % N, src // N]
            for gi in range(NGLOB):
                kb[pl.ds((6 + gi) * BLK, BLK)] = gk[gi * HEADS + h]
                vb[pl.ds((6 + gi) * BLK, BLK)] = gv[gi * HEADS + h]
            kall, vall = kb[...], vb[...]
            qb, gb = q[rows, cols], g[rows, cols]
            s = lax.dot_general(qb, kall, ROWS_T, preferred_element_type=F32) * scale
            key_id = lax.broadcasted_iota(jnp.int32, (BLK, key_count), 1)
            if b == 0:
                bad = (key_id < BLK) & (me == 0)
            else:
                bad = (key_id >= 2 * BLK) & (key_id < 3 * BLK) & (me == total - 1)
            s = jnp.where(bad, -jnp.inf, s)
            m = jnp.max(s, -1, keepdims=True)
            e = jnp.exp(s - m)
            p = e * (1.0 / jnp.sum(e, -1, keepdims=True))
            plow = p.astype(BF16)
            o = lax.dot_general(plow, vall, (((1,), (0,)), ((), ())), preferred_element_type=F32).astype(BF16)
            delta = jnp.sum(gb.astype(F32) * o.astype(F32), -1, keepdims=True)
            dp = lax.dot_general(gb, vall, ROWS_T, preferred_element_type=F32)
            ds = (scale * p * (dp - delta)).astype(BF16)
            att[rows, cols] = o
            dq[rows, cols] = lax.dot_general(
                ds, kall, (((1,), (0,)), ((), ())), preferred_element_type=F32
            ).astype(BF16)
            for lhs, rhs, win, term, gacc in ((ds, qb, wk, termk, gak), (plow, gb, wv, termv, gav)):
                t = lax.dot_general(lhs, rhs, COLS_T, preferred_element_type=F32)
                if b == 0:
                    win[pl.ds(0, 3 * BLK), cols] = t[: 3 * BLK]
                else:
                    win[pl.ds(BLK, 2 * BLK), cols] += t[: 2 * BLK]
                    win[pl.ds(3 * BLK, BLK), cols] = t[2 * BLK : 3 * BLK]
                for r in range(NRAND):
                    term[(h * NRAND + r) * 2 + b] = t[(3 + r) * BLK : (4 + r) * BLK].astype(BF16)
                for gi in range(NGLOB):
                    piece = t[(6 + gi) * BLK : (7 + gi) * BLK]
                    if b == 0:
                        gacc[gi * HEADS + h] = piece
                    else:
                        gacc[gi * HEADS + h] += piece
        return carry

    lax.fori_loop(0, HEADS, head, 0)

    def fill_back(dst_k, dst_v, zd, yd):
        for s in range(N):
            dst_k[s] = termk[tab[INV + zd * N + s]]
            dst_v[s] = termv[tab[INV + s * N + yd]]
        dst_k[N] = gak[zd].astype(BF16)
        dst_v[N] = gav[yd].astype(BF16)

    hsk[0] = wk[pl.ds(0, BLK)].astype(BF16)
    hsk[1] = wk[pl.ds(3 * BLK, BLK)].astype(BF16)
    hsv[0] = wv[pl.ds(0, BLK)].astype(BF16)
    hsv[1] = wv[pl.ds(3 * BLK, BLK)].astype(BF16)

    def back(j, carry):
        d = far_first(j)
        zd = (z + d) % N
        yd = (y + d) % N
        fill_back(rsk.at[j], rsv.at[j], zd, yd)
        rc(rsk.at[j], rrk.at[z], rb_s.at[0, j], rb_r.at[0, j], zd * N + y).start()
        rc(rsv.at[j], rrv.at[y], rb_s.at[1, j], rb_r.at[1, j], z * N + yd).start()
        return carry

    lax.fori_loop(0, N - 1, back, 0)
    fill_back(rrk.at[z], rrv.at[y], z, y)
    halo_back = [
        rc(hsk.at[0], hrk.at[1], hb_s.at[0], hb_r.at[0], left_seq),
        rc(hsk.at[1], hrk.at[0], hb_s.at[1], hb_r.at[1], right_seq),
        rc(hsv.at[0], hrv.at[1], hb_s.at[2], hb_r.at[2], left_seq),
        rc(hsv.at[1], hrv.at[0], hb_s.at[3], hb_r.at[3], right_seq),
    ]
    for c_ in halo_back:
        c_.start()

    def back_wait(j, carry):
        d = far_first(j)
        zs = (z + N - d) % N
        ys = (y + N - d) % N
        rc(rsk.at[j], rrk.at[zs], rb_s.at[0, j], rb_r.at[0, j], zs * N + y).wait_recv()
        rc(rsv.at[j], rrv.at[ys], rb_s.at[1, j], rb_r.at[1, j], z * N + ys).wait_recv()
        return carry

    lax.fori_loop(0, N - 1, back_wait, 0)

    def total_of(read):
        acc = read(0).astype(F32)
        for s in range(1, N):
            acc += read(s).astype(F32)
        return acc.astype(BF16)

    g2k[y] = total_of(lambda s: rrk[s, N])
    g2v[z] = total_of(lambda s: rrv[s, N])
    small(g2k, g2v, g2_s, g2_r, "y", "z")

    tile = 16

    def partial(rel):
        for buf, part, base, p in ((rrk, pk, CODE_K, y), (rrv, pv, CODE_V, z)):
            tgt = (p + rel) % N
            weight = []
            for s in range(N):
                code = tab[base + s * N + tgt]
                weight.append([jnp.where(code == i, 1.0, 0.0).astype(F32) for i in range(ITEMS)])

            def rows_step(i, carry, buf=buf, part=part, tgt=tgt, weight=weight):
                rows = pl.ds(pl.multiple_of(i * tile, tile), tile)
                acc = [None] * ITEMS
                for s in range(N):
                    x = buf[s, tgt, rows].astype(F32)
                    for c in range(ITEMS):
                        w = x * weight[s][c]
                        acc[c] = w if acc[c] is None else acc[c] + w
                for c in range(ITEMS):
                    part[tgt, c, rows] = acc[c]
                return carry

            lax.fori_loop(0, BLK // tile, rows_step, 0)

    rs_index = {key: i for i, key in enumerate(RS)}

    def rs_copy(arr, i):
        f, s = RS[i]
        return rc(rsend.at[arr, i], rrecv.at[arr, i], rs_s.at[arr, i], rs_r.at[arr, i],
                  dev(("y", "z")[arr], FLOWS[f][0]))

    def rs_send(f, s):
        dr, c, hops = FLOWS[f]
        i = rs_index[(f, s)]
        for arr, part, p in ((0, pk, y), (1, pv, z)):
            tgt = (p + dr * (hops - s + 1) + N) % N
            x = part[tgt, pl.ds(c * HEADS, HEADS)]
            if s > 1:
                j = rs_index[(f, s - 1)]
                rs_copy(arr, j).wait_recv()
                x = x + rrecv[arr, j].astype(F32)
            rsend[arr, i] = x.astype(BF16)
            rs_copy(arr, i).start()

    def step_loop(first, stride, count):
        def body(j, carry):
            partial(first + stride * j)
            return carry

        lax.fori_loop(0, count, body, 0)

    step_loop(3, 1, 3)
    for f in range(4):
        rs_send(f, 1)
    step_loop(2, 4, 2)
    for f in range(4):
        rs_send(f, 2)
    small_wait(g2k, g2v, g2_s, g2_r, "y", "z")
    g3k[z] = total_of(lambda s: g2k[s])
    g3v[y] = total_of(lambda s: g2v[s])
    small(g3k, g3v, g3_s, g3_r, "z", "y")
    step_loop(0, 1, 2)
    step_loop(7, 1, 1)
    for f in range(4):
        rs_send(f, 3)
    for f in range(2):
        rs_send(f, 4)
    for c_ in halo_back:
        c_.wait_recv()
    small_wait(g3k, g3v, g3_s, g3_r, "z", "y")

    for f in (2, 3, 0, 1):
        for arr in (0, 1):
            rs_copy(arr, rs_index[(f, FLOWS[f][2])]).wait_recv()
    for arr, part, p, win, hr, g3, out in (
        (0, pk, y, wk, hrk, g3k, dk),
        (1, pv, z, wv, hrv, g3v, dv),
    ):
        for b in range(2):
            flows = [f for f in range(4) if FLOWS[f][1] == b]
            for h in range(HEADS):
                cols = pl.ds(h * HD, HD)
                x = win[pl.ds((1 + b) * BLK, BLK), cols] + hr[b, :, cols].astype(F32)
                x += part[p, b * HEADS + h]
                for f in flows:
                    x += rrecv[arr, rs_index[(f, FLOWS[f][2])], h].astype(F32)
                for gi in range(NGLOB):
                    mine = jnp.where(gblk[gi] == me * 2 + b, 1.0, 0.0).astype(F32)
                    x += g3[gi * HEADS + h].astype(F32) * mine
                out[pl.ds(b * BLK, BLK), cols] = x.astype(BF16)

    for arr in (0, 1):
        for i in range(len(AG)):
            ag_copy(arr, i).wait_send()
        for i in range(len(RS)):
            rs_copy(arr, i).wait_send()
    for c_ in halo + halo_back:
        c_.wait_send()

    def drain(j, carry):
        for a, (bk, bv) in ((b_s, (sk, sv)), (rb_s, (rsk, rsv))):
            rc(bk.at[j], rk.at[z], a.at[0, j], b_r.at[0, j], me).wait_send()
            rc(bv.at[j], rv.at[y], a.at[1, j], b_r.at[1, j], me).wait_send()
        for a, (bk, bv), (ik, iv) in (
            (gg_s, (gk, gv), (y, z)),
            (g2_s, (g2k, g2v), (y, z)),
            (g3_s, (g3k, g3v), (z, y)),
        ):
            rc(bk.at[ik], bk.at[ik], a.at[0, j], gg_r.at[0, j], me).wait_send()
            rc(bv.at[iv], bv.at[iv], a.at[1, j], gg_r.at[1, j], me).wait_send()
        return carry

    lax.fori_loop(0, N - 1, drain, 0)


def tables(random_blocks, global_blocks):
    me = lax.axis_index("seq")
    z, y = me // N, me % N
    lists = random_blocks.reshape(HEADS * NRAND, N, N, 2)
    head = (jnp.arange(HEADS * NRAND, dtype=jnp.int32) // NRAND)[:, None, None]
    span = jnp.arange(N, dtype=jnp.int32)

    def codes(rows, owner_ids):
        owner = rows // 2
        code = rows % 2 * HEADS + head + 1
        hit = owner[..., None] == owner_ids
        return jnp.sum(jnp.where(hit, code[..., None], 0), (0, 2)).reshape(N * N) - 1

    code_k = codes(lax.dynamic_index_in_dim(lists, y, 2, keepdims=False), z * N + span)
    code_v = codes(lax.dynamic_index_in_dim(lists, z, 1, keepdims=False), span * N + y)
    mine = lax.dynamic_index_in_dim(
        lax.dynamic_index_in_dim(lists, z, 1, keepdims=False), y, 1, keepdims=False
    ).reshape(HEADS * NRAND * 2)
    order = jnp.arange(HEADS * NRAND * 2, dtype=jnp.int32)
    hit = (mine // 2)[:, None] == jnp.arange(N * N, dtype=jnp.int32)[None, :]
    inv = jnp.sum(jnp.where(hit, order[:, None], 0), 0)
    return jnp.concatenate([code_k, code_v, inv, mine, global_blocks]).astype(jnp.int32)


def body(queries, keys, values, out_grad, random_blocks, global_blocks):
    tab = tables(random_blocks, global_blocks)
    full = jax.ShapeDtypeStruct(queries.shape, BF16)
    vm, dma = pltpu.VMEM, pltpu.SemaphoreType.DMA
    bund = lambda n: vm((n, SLOTS, BLK, HD), BF16)
    keys_n = (3 + NRAND + NGLOB) * BLK
    scratch = [
        vm((N, ITEMS, BLK, HD), BF16), vm((N, ITEMS, BLK, HD), BF16),
        vm((4 * BLK, HEADS * HD), BF16), vm((4 * BLK, HEADS * HD), BF16),
        bund(N - 1), bund(N - 1), bund(N), bund(N),
        vm((N, BLK, HD), BF16), vm((N, BLK, HD), BF16),
        vm((2, keys_n, HD), BF16), vm((2, keys_n, HD), BF16),
        vm((24, BLK, HD), BF16), vm((24, BLK, HD), BF16),
        vm((4 * BLK, HEADS * HD), F32), vm((4 * BLK, HEADS * HD), F32),
        vm((N, BLK, HD), F32), vm((N, BLK, HD), F32),
        vm((2, BLK, HEADS * HD), BF16), vm((2, BLK, HEADS * HD), BF16),
        vm((2, BLK, HEADS * HD), BF16), vm((2, BLK, HEADS * HD), BF16),
        bund(N - 1), bund(N - 1), bund(N), bund(N),
        vm((N, ITEMS, BLK, HD), F32), vm((N, ITEMS, BLK, HD), F32),
        vm((N, BLK, HD), BF16), vm((N, BLK, HD), BF16),
        vm((N, BLK, HD), BF16), vm((N, BLK, HD), BF16),
        vm((2, len(RS), HEADS, BLK, HD), BF16), vm((2, len(RS), HEADS, BLK, HD), BF16),
        dma((2 * ITEMS + 2,)), dma((2, len(AG))), dma((2, len(AG))), dma((4,)), dma((4,)),
        dma((2, N - 1)), dma((2, N - 1)), dma((2, N - 1)), dma((2, N - 1)),
        dma((4,)), dma((4,)), dma((2, N - 1)), dma((2, N - 1)),
        dma((2, N - 1)), dma((2, N - 1)), dma((2, N - 1)), dma((2, N - 1)),
        dma((2, len(RS))), dma((2, len(RS))),
    ]
    spec = pl.BlockSpec(memory_space=pltpu.VMEM)
    return pl.pallas_call(
        kernel,
        out_shape=(full,) * 4,
        in_specs=[pl.BlockSpec(memory_space=pltpu.SMEM)] + [spec] * 4,
        out_specs=(spec,) * 4,
        scratch_shapes=scratch,
        compiler_params=pltpu.CompilerParams(collective_id=0, has_side_effects=True),
    )(tab, queries, keys, values, out_grad)


def solution(mesh):
    wide = P(("dp", "seq"), "heads")
    return jax.shard_map(
        body,
        mesh=mesh,
        in_specs=(wide, wide, wide, wide, P(("dp", "heads"), None, None), P("dp")),
        out_specs=(wide,) * 4,
        check_vma=False,
    )
```

time: 464 us -> 137 us (0.30)
  waiting for transfers between devices: 355 us -> 0 us
  Pallas kernels: 0 us -> 129 us
  starting transfers between devices: 44.5 us -> 0 us
  between operations: 19.7 us -> 0.82 us
  local copies, waits for them, and re-layouts: 25.5 us -> 6.76 us
  matrix products: 9.08 us -> 0 us
  other arithmetic: 9.02 us -> 0.71 us
    psum x2 -> x0, waiting for transfers between devices: 282 us -> none  [the longest x1 143 us: from_root(): return lax.psum(kept, axis)]
    pallas_call x0 -> x1, Pallas kernels: none -> 129 us  [body(): pl.pallas_call(kernel, out_shape=(full,) * 4, in_specs=[pl.BlockSpec(memo...]
    ppermute x4 -> x0, waiting for transfers between devices: 68.6 us -> none  [the longest x2 68.6 us: with_halo(): lax.ppermute(head, axis, [((i + 1) % count, i) for i in range(ends)])]
    all_to_all x2 -> x0, starting transfers between devices: 31.8 us -> none  [the longest x1 23.6 us: body(): lax.all_to_all(outgoing, 'seq', split_axis=0, concat_axis=0, tiled=True)]
    ppermute x4 -> x0, starting transfers between devices: 12.3 us -> none  [the longest x2 9.76 us: with_halo(): lax.ppermute(tail, axis, [(i, (i + 1) % count) for i in range(ends)])]
    dot_general x10 -> x0, matrix products: 9.08 us -> none  [the longest x1 2.98 us: body(): jnp.einsum('sbh,scrd->cbrhd', selector, returned, preferred_element_type=...]
    convert_element_type x5 -> x0, local copies, waits for them, and re-layouts: 5.78 us -> none  [the longest x1 2.7 us: body(): parcel = jnp.einsum('sbrh,cbrjhd->scjd', placement, random_back, preferre...]
    all_to_all x2 -> x0, waiting for transfers between devices: 4.93 us -> none  [the longest x1 4.93 us: body(): lax.all_to_all(parcel, 'seq', split_axis=0, concat_axis=0, tiled=True)]
  transfers between devices with their start and end apart: 8 -> 0, of which waited for: 5 -> 0; matrix products, arithmetic and copies ran while one was open for 4% -> 0% of each run, Pallas kernels for 0% -> 0%
where the time goes in v1:
time: 137 us
  Pallas kernels  129 us (94%)
  local copies, waits for them, and re-layouts  6.76 us (5%)
    pallas_call x1, Pallas kernels, body(): pl.pallas_call(kernel, out_shape=(full,) * 4, in_specs=[pl.BlockSpec(memo...  129 us
    unnamed x15, local copies, waits for them, and re-layouts  5.54 us

profile of v1, /device:TPU:14, one launch (start us, length us, event | category | flops | bytes accessed | tf_op | source)
XLA Modules:
  0.0 136.9 jit_solution(14813804714099888548)
XLA Ops:
  0.7 0.0 copy-start.3
  0.7 0.6 copy-done.3
  1.4 0.2 copy.37
  1.5 0.2 reshape.177
  1.7 0.1 copy.44
  1.8 0.1 reshape.178
  1.9 0.1 select_reduce_fusion.2
  2.1 0.3 select_reduce_fusion
  2.4 0.1 sub.41
  2.5 0.3 select_reduce_fusion.1
  2.8 0.0 copy-start.4
  2.8 0.1 sub.38
  2.9 0.6 copy-done.4
  3.5 0.6 concatenate.3.tab
  4.1 128.6 %shard_map.93 = (bf16[128,512]{1,0:T(8,128)(2,1)}, bf16[128,512]{1,0:T(8,128)(2,1)}, bf16[128,512]{1,0:T(8,128)(2,1)}, bf16[128,512]{1,0:T(8,128)(2,1)}) custom-call(s32[218]{0:T(256)} %concatenate.3.tab, bf16[128,512]{1,0:T(8,128)(2,1)} %q.1, bf16[128,512]{1,0:T(8,128)(2,1)} %k.1, bf16[128,512]{1,0:T(8,128)(2,1)} %v.1, bf16[128,512]{1,0:T(8,128)(2,1)} %g.1), custom_call_target="tpu_custom_call" | custom-call | tf_op jit(solution)/shard_map/pallas_call | solution.py:469
  132.7 0.0 copy-start.2
  132.7 1.6 %copy.87 = bf16[128,512]{1,0:T(8,128)(2,1)} copy(bf16[128,512]{1,0:T(8,128)(2,1)} %get-tuple-element.14) | data formatting | bytes 262144
  134.3 0.0 copy-done.2
  134.3 0.0 copy-start.1
  134.3 0.7 copy.88
  135.0 0.3 copy-done.1
  135.3 0.0 copy-start
  135.3 0.7 copy.89
  136.0 0.3 copy-done
  136.2 0.7 copy.90
  (14 shorter events, 0.1 us)
Async XLA Ops:
  0.7 0.7 copy-start.3
  2.8 0.7 copy-start.4
  132.7 1.6 %copy-start.2 = (bf16[128,512]{1,0:T(8,128)(2,1)S(1)}, bf16[128,512]{1,0:T(8,128)(2,1)}, u32[]{:S(2)}) copy-start(bf16[128,512]{1,0:T(8,128)(2,1)} %get-tuple-element.15) | copy-start | bytes 393220
  134.3 1.0 copy-start.1
  135.3 1.0 copy-start

commit v2 on v1

--- a/solution.py
+++ b/solution.py
@@ -13,8 +13,6 @@
 NRAND = 3
 NGLOB = 2
 ITEMS = 2 * HEADS
-CODE_K, CODE_V, INV, SRC, GLB = 0, 64, 128, 192, 216
-SLOTS = N + 1
 F32 = jnp.float32
 BF16 = jnp.bfloat16
 ROWS_T = (((1,), (1,)), ((), ()))
@@ -26,13 +24,15 @@
 
 
 def kernel(
-    tab, q, k, v, g,
+    glb, lists, q_hbm, k, v, g_hbm,
     att, dq, dk, dv,
+    q, g, rbv, rbs,
+    tvm, tsm, gsk, gsv, gck, gcv,
     agk, agv, wink, winv, sk, sv, rk, rv, gk, gv,
     ka, va, termk, termv, wk, wv, gak, gav, hsk, hsv, hrk, hrv,
     rsk, rsv, rrk, rrv, pk, pv, g2k, g2v, g3k, g3v,
     rsend, rrecv,
-    lsem, ag_s, ag_r, h_s, h_r, b_s, b_r, gg_s, gg_r,
+    tsem, gc_s, gc_r, lsem, ag_s, ag_r, h_s, h_r, b_s, b_r, gg_s, gg_r,
     hb_s, hb_r, rb_s, rb_r, g2_s, g2_r, g3_s, g3_r, rs_s, rs_r,
 ):
     me = lax.axis_index("seq")
@@ -61,7 +61,15 @@
         pltpu.make_async_copy(k, wink.at[pl.ds(BLK, 2 * BLK)], lsem.at[2 * ITEMS]),
         pltpu.make_async_copy(v, winv.at[pl.ds(BLK, 2 * BLK)], lsem.at[2 * ITEMS + 1]),
     ]
-    for c in locals_ + win_own:
+    list_copies = [
+        pltpu.make_async_copy(lists, rbv, lsem.at[2 * ITEMS + 2]),
+        pltpu.make_async_copy(lists, rbs, lsem.at[2 * ITEMS + 3]),
+    ]
+    query_copies = [
+        pltpu.make_async_copy(q_hbm, q, lsem.at[2 * ITEMS + 4]),
+        pltpu.make_async_copy(g_hbm, g, lsem.at[2 * ITEMS + 5]),
+    ]
+    for c in list_copies + locals_ + win_own + query_copies:
         c.start()
 
     barrier = pltpu.get_barrier_semaphore()
@@ -76,8 +84,22 @@
     lax.fori_loop(1, N, greet, 0)
     pl.semaphore_signal(barrier, inc=1, device_id={"seq": right_seq}, device_id_type=MESH)
     pl.semaphore_signal(barrier, inc=1, device_id={"seq": left_seq}, device_id_type=MESH)
+    for c in list_copies:
+        c.wait()
+    src_ids = lax.broadcasted_iota(jnp.int32, (N * N, 2 * N * N), 0)
+    parity = lax.broadcasted_iota(jnp.int32, (1, 2 * N * N), 1) % 2
+    want = jnp.zeros((N * N, 2 * N * N), jnp.int32)
+    for h in range(HEADS):
+        for r in range(NRAND):
+            row = rbv[r, pl.ds(h, 1), :]
+            entry = row % 2 * HEADS + (h + 1 + 16 * (2 * (h * NRAND + r))) + 16 * parity
+            want = jnp.maximum(want, jnp.where(row // 2 == src_ids, entry, 0))
+    tvm[...] = want
+
     for c in locals_:
         c.wait()
+    to_scalars = pltpu.make_async_copy(tvm, tsm, tsem)
+    to_scalars.start()
     pl.semaphore_wait(barrier, 2 * N)
 
     def ag_copy(arr, i):
@@ -116,13 +138,17 @@
         if i == 3:
             for c_ in halo:
                 c_.start()
-    for c in win_own:
+    for c in win_own + query_copies:
         c.wait()
+    to_scalars.wait()
+
+    def entry_of(s, dest):
+        return jnp.maximum(tsm[s, 2 * dest], tsm[s, 2 * dest + 1])
 
     def item(buf, slot, code):
         return buf[slot, code]
 
-    gblk = [tab[GLB + i] for i in range(NGLOB)]
+    gblk = [glb[i] for i in range(NGLOB)]
 
     def pick(idx):
         return jnp.where(idx // HEADS == 0, gblk[0], gblk[1])
@@ -130,14 +156,28 @@
     def far_first(j):
         return jnp.where(j % 2 == 1, N // 2 - (j + 1) // 2, N // 2 + j // 2)
 
+    blk = pick(y)
+    gsk[...] = item(agk, blk // 2 % N, blk % 2 * HEADS + y % HEADS)
+    gck[z] = gsk[...]
+    blk = pick(z)
+    gsv[...] = item(agv, blk // (2 * N), blk % 2 * HEADS + z % HEADS)
+    gcv[y] = gsv[...]
+
+    def eighth(j, carry):
+        d = far_first(j)
+        rc(gsk, gck.at[z], gc_s.at[0, j], gc_r.at[0, j], dev("z", d)).start()
+        rc(gsv, gcv.at[y], gc_s.at[1, j], gc_r.at[1, j], dev("y", d)).start()
+        return carry
+
+    lax.fori_loop(0, N - 1, eighth, 0)
+
+    def code_of(s, dest):
+        return jnp.maximum(entry_of(s, dest) % 16 - 1, 0)
+
     def fill(dst_k, dst_v, zd, yd):
         for s in range(N):
-            dst_k[s] = item(agk, s, jnp.maximum(tab[CODE_K + zd * N + s], 0))
-            dst_v[s] = item(agv, s, jnp.maximum(tab[CODE_V + yd * N + s], 0))
-        blk = pick(y)
-        dst_k[N] = item(agk, blk // 2 % N, blk % 2 * HEADS + y % HEADS)
-        blk = pick(z)
-        dst_v[N] = item(agv, blk // (2 * N), blk % 2 * HEADS + z % HEADS)
+            dst_k[s] = item(agk, s, code_of(z * N + s, zd * N + y))
+            dst_v[s] = item(agv, s, code_of(s * N + y, z * N + yd))
 
     def bundle(j, carry):
         d = far_first(j)
@@ -151,18 +191,13 @@
     lax.fori_loop(0, N - 1, bundle, 0)
     fill(rk.at[z], rv.at[y], z, y)
 
-    def bundle_wait(j, carry):
+    def eighth_wait(j, carry):
         d = far_first(j)
         zs = (z + N - d) % N
         ys = (y + N - d) % N
-        rc(sk.at[j], rk.at[zs], b_s.at[0, j], b_r.at[0, j], zs * N + y).wait_recv()
-        rc(sv.at[j], rv.at[ys], b_s.at[1, j], b_r.at[1, j], z * N + ys).wait_recv()
-        return carry
-
-    lax.fori_loop(0, N - 1, bundle_wait, 0)
-
-    gk[y] = rk[pick(y) // (2 * N), N]
-    gv[z] = rv[pick(z) // 2 % N, N]
+        rc(gsk, gck.at[zs], gc_s.at[0, j], gc_r.at[0, j], zs * N + y).wait_recv()
+        rc(gsv, gcv.at[ys], gc_s.at[1, j], gc_r.at[1, j], z * N + ys).wait_recv()
+        return carry
 
     def small(src_k, src_v, ss, rs, axis_k, axis_v):
         def start(j, carry):
@@ -184,9 +219,22 @@
 
         lax.fori_loop(0, N - 1, wait, 0)
 
+    lax.fori_loop(0, N - 1, eighth_wait, 0)
+    gk[y] = gck[pick(y) // (2 * N)]
+    gv[z] = gcv[pick(z) // 2 % N]
     small(gk, gv, gg_s, gg_r, "y", "z")
     for c_ in halo:
         c_.wait_recv()
+
+    def bundle_wait(j, carry):
+        d = far_first(j)
+        zs = (z + N - d) % N
+        ys = (y + N - d) % N
+        rc(sk.at[j], rk.at[zs], b_s.at[0, j], b_r.at[0, j], zs * N + y).wait_recv()
+        rc(sv.at[j], rv.at[ys], b_s.at[1, j], b_r.at[1, j], z * N + ys).wait_recv()
+        return carry
+
+    lax.fori_loop(0, N - 1, bundle_wait, 0)
     small_wait(gk, gv, gg_s, gg_r, "y", "z")
 
     scale = HD ** (-0.5)
@@ -200,7 +248,7 @@
             kb[pl.ds(0, 3 * BLK)] = wink[pl.ds(b * BLK, 3 * BLK), cols]
             vb[pl.ds(0, 3 * BLK)] = winv[pl.ds(b * BLK, 3 * BLK), cols]
             for r in range(NRAND):
-                src = tab[SRC + (h * NRAND + r) * 2 + b] // 2
+                src = rbs[r, h, 2 * me + b] // 2
                 kb[pl.ds((3 + r) * BLK, BLK)] = rk[src // N, src % N]
                 vb[pl.ds((3 + r) * BLK, BLK)] = rv[src % N, src // N]
             for gi in range(NGLOB):
@@ -248,8 +296,8 @@
 
     def fill_back(dst_k, dst_v, zd, yd):
         for s in range(N):
-            dst_k[s] = termk[tab[INV + zd * N + s]]
-            dst_v[s] = termv[tab[INV + s * N + yd]]
+            dst_k[s] = termk[entry_of(zd * N + s, me) // 16]
+            dst_v[s] = termv[entry_of(s * N + yd, me) // 16]
         dst_k[N] = gak[zd].astype(BF16)
         dst_v[N] = gav[yd].astype(BF16)
 
@@ -301,12 +349,15 @@
     tile = 16
 
     def partial(rel):
-        for buf, part, base, p in ((rrk, pk, CODE_K, y), (rrv, pv, CODE_V, z)):
+        for buf, part, p in ((rrk, pk, y), (rrv, pv, z)):
             tgt = (p + rel) % N
             weight = []
             for s in range(N):
-                code = tab[base + s * N + tgt]
-                weight.append([jnp.where(code == i, 1.0, 0.0).astype(F32) for i in range(ITEMS)])
+                if buf is rrk:
+                    code = entry_of(z * N + tgt, s * N + y) % 16
+                else:
+                    code = entry_of(tgt * N + y, z * N + s) % 16
+                weight.append([jnp.where(code == i + 1, 1.0, 0.0).astype(F32) for i in range(ITEMS)])
 
             def rows_step(i, carry, buf=buf, part=part, tgt=tgt, weight=weight):
                 rows = pl.ds(pl.multiple_of(i * tile, tile), tile)
@@ -408,45 +459,33 @@
         ):
             rc(bk.at[ik], bk.at[ik], a.at[0, j], gg_r.at[0, j], me).wait_send()
             rc(bv.at[iv], bv.at[iv], a.at[1, j], gg_r.at[1, j], me).wait_send()
+        rc(gsk, gck.at[z], gc_s.at[0, j], gc_r.at[0, j], me).wait_send()
+        rc(gsv, gcv.at[y], gc_s.at[1, j], gc_r.at[1, j], me).wait_send()
         return carry
 
     lax.fori_loop(0, N - 1, drain, 0)
 
 
-def tables(random_blocks, global_blocks):
-    me = lax.axis_index("seq")
-    z, y = me // N, me % N
-    lists = random_blocks.reshape(HEADS * NRAND, N, N, 2)
-    head = (jnp.arange(HEADS * NRAND, dtype=jnp.int32) // NRAND)[:, None, None]
-    span = jnp.arange(N, dtype=jnp.int32)
-
-    def codes(rows, owner_ids):
-        owner = rows // 2
-        code = rows % 2 * HEADS + head + 1
-        hit = owner[..., None] == owner_ids
-        return jnp.sum(jnp.where(hit, code[..., None], 0), (0, 2)).reshape(N * N) - 1
-
-    code_k = codes(lax.dynamic_index_in_dim(lists, y, 2, keepdims=False), z * N + span)
-    code_v = codes(lax.dynamic_index_in_dim(lists, z, 1, keepdims=False), span * N + y)
-    mine = lax.dynamic_index_in_dim(
-        lax.dynamic_index_in_dim(lists, z, 1, keepdims=False), y, 1, keepdims=False
-    ).reshape(HEADS * NRAND * 2)
-    order = jnp.arange(HEADS * NRAND * 2, dtype=jnp.int32)
-    hit = (mine // 2)[:, None] == jnp.arange(N * N, dtype=jnp.int32)[None, :]
-    inv = jnp.sum(jnp.where(hit, order[:, None], 0), 0)
-    return jnp.concatenate([code_k, code_v, inv, mine, global_blocks]).astype(jnp.int32)
+def settle(*refs):
+    for src, dst in zip(refs[:4], refs[4:]):
+        dst[...] = src[...]
 
 
 def body(queries, keys, values, out_grad, random_blocks, global_blocks):
-    tab = tables(random_blocks, global_blocks)
+    lists = random_blocks.transpose(1, 0, 2)
     full = jax.ShapeDtypeStruct(queries.shape, BF16)
     vm, dma = pltpu.VMEM, pltpu.SemaphoreType.DMA
-    bund = lambda n: vm((n, SLOTS, BLK, HD), BF16)
+    bund = lambda n, slots: vm((n, slots, BLK, HD), BF16)
     keys_n = (3 + NRAND + NGLOB) * BLK
+    small = vm((N, BLK, HD), BF16)
     scratch = [
+        vm(queries.shape, BF16), vm(queries.shape, BF16),
+        vm(lists.shape, jnp.int32), pltpu.SMEM(lists.shape, jnp.int32),
+        vm((N * N, 2 * N * N), jnp.int32), pltpu.SMEM((N * N, 2 * N * N), jnp.int32),
+        vm((BLK, HD), BF16), vm((BLK, HD), BF16), small, small,
         vm((N, ITEMS, BLK, HD), BF16), vm((N, ITEMS, BLK, HD), BF16),
         vm((4 * BLK, HEADS * HD), BF16), vm((4 * BLK, HEADS * HD), BF16),
-        bund(N - 1), bund(N - 1), bund(N), bund(N),
+        bund(N - 1, N), bund(N - 1, N), bund(N, N), bund(N, N),
         vm((N, BLK, HD), BF16), vm((N, BLK, HD), BF16),
         vm((2, keys_n, HD), BF16), vm((2, keys_n, HD), BF16),
         vm((24, BLK, HD), BF16), vm((24, BLK, HD), BF16),
@@ -454,26 +493,33 @@
         vm((N, BLK, HD), F32), vm((N, BLK, HD), F32),
         vm((2, BLK, HEADS * HD), BF16), vm((2, BLK, HEADS * HD), BF16),
         vm((2, BLK, HEADS * HD), BF16), vm((2, BLK, HEADS * HD), BF16),
-        bund(N - 1), bund(N - 1), bund(N), bund(N),
+        bund(N - 1, N + 1), bund(N - 1, N + 1), bund(N, N + 1), bund(N, N + 1),
         vm((N, ITEMS, BLK, HD), F32), vm((N, ITEMS, BLK, HD), F32),
         vm((N, BLK, HD), BF16), vm((N, BLK, HD), BF16),
         vm((N, BLK, HD), BF16), vm((N, BLK, HD), BF16),
         vm((2, len(RS), HEADS, BLK, HD), BF16), vm((2, len(RS), HEADS, BLK, HD), BF16),
-        dma((2 * ITEMS + 2,)), dma((2, len(AG))), dma((2, len(AG))), dma((4,)), dma((4,)),
+        dma, dma((2, N - 1)), dma((2, N - 1)), dma((2 * ITEMS + 6,)), dma((2, len(AG))), dma((2, len(AG))), dma((4,)), dma((4,)),
         dma((2, N - 1)), dma((2, N - 1)), dma((2, N - 1)), dma((2, N - 1)),
         dma((4,)), dma((4,)), dma((2, N - 1)), dma((2, N - 1)),
         dma((2, N - 1)), dma((2, N - 1)), dma((2, N - 1)), dma((2, N - 1)),
         dma((2, len(RS))), dma((2, len(RS))),
     ]
     spec = pl.BlockSpec(memory_space=pltpu.VMEM)
-    return pl.pallas_call(
+    smem = pl.BlockSpec(memory_space=pltpu.SMEM)
+    outs = pl.pallas_call(
         kernel,
         out_shape=(full,) * 4,
-        in_specs=[pl.BlockSpec(memory_space=pltpu.SMEM)] + [spec] * 4,
+        in_specs=[smem] + [pl.BlockSpec(memory_space=pltpu.MemorySpace.HBM)] * 5,
         out_specs=(spec,) * 4,
         scratch_shapes=scratch,
         compiler_params=pltpu.CompilerParams(collective_id=0, has_side_effects=True),
-    )(tab, queries, keys, values, out_grad)
+    )(global_blocks, lists, queries, keys, values, out_grad)
+    return pl.pallas_call(
+        settle,
+        out_shape=(full,) * 4,
+        in_specs=[spec] * 4,
+        out_specs=(spec,) * 4,
+    )(*outs)
 
 
 def solution(mesh):

time: 137 us -> 130 us (0.949)
  local copies, waits for them, and re-layouts: 6.76 us -> 0 us
    unnamed x15 -> x0, local copies, waits for them, and re-layouts: 5.54 us -> none
    pallas_call x1 -> x2, Pallas kernels: 129 us -> 129 us  [the longest x1 127 us: body(): pl.pallas_call(kernel, out_shape=(full,) * 4, in_specs=[smem] + [pl.Block...]
where the time goes in v2:
time: 130 us
  Pallas kernels  129 us (99%)
    pallas_call x1, Pallas kernels, body(): pl.pallas_call(kernel, out_shape=(full,) * 4, in_specs=[smem] + [pl.Block...  127 us

profile of v2, /device:TPU:14, one launch (start us, length us, event | category | flops | bytes accessed | tf_op | source)
XLA Modules:
  0.0 130.0 jit_solution(6005388952946516066)
XLA Ops:
  0.6 127.4 %shard_map.93 = (bf16[128,512]{1,0:T(8,128)(2,1)}, bf16[128,512]{1,0:T(8,128)(2,1)}, bf16[128,512]{1,0:T(8,128)(2,1)}, bf16[128,512]{1,0:T(8,128)(2,1)}) custom-call(s32[2]{0:T(128)} %glb.1, s32[3,4,128]{2,1,0:T(4,128)} %bitcast.1, bf16[128,512]{1,0:T(8,128)(2,1)} %q_hbm.1, bf16[128,512]{1,0:T(8,128)(2,1)} %k.1, bf16[128,512]{1,0:T(8,128)(2,1)} %v.1, ...), custom_call_target="tpu_custom_call" | custom-call | tf_op jit(solution)/shard_map/pallas_call | solution.py:509
  128.1 1.9 %shard_map.94 = (bf16[128,512]{1,0:T(8,128)(2,1)}, bf16[128,512]{1,0:T(8,128)(2,1)}, bf16[128,512]{1,0:T(8,128)(2,1)}, bf16[128,512]{1,0:T(8,128)(2,1)}) custom-call(bf16[128,512]{1,0:T(8,128)(2,1)} %get-tuple-element.8.refs_0_, bf16[128,512]{1,0:T(8,128)(2,1)} %get-tuple-element.9.refs_1_, bf16[128,512]{1,0:T(8,128)(2,1)} %get-tuple-element.10.refs_2_, ...), custom_call_target="tpu_custom_call" | custom-call | tf_op jit(solution)/shard_map/pallas_call | solution.py:517

commit v3 on v2

--- a/solution.py
+++ b/solution.py
@@ -28,11 +28,12 @@
     att, dq, dk, dv,
     q, g, rbv, rbs,
     tvm, tsm, gsk, gsv, gck, gcv,
-    agk, agv, wink, winv, sk, sv, rk, rv, gk, gv,
-    ka, va, termk, termv, wk, wv, gak, gav, hsk, hsv, hrk, hrv,
+    agk, agv, winv, sk, sv, rk, rv, gk, gv,
+    ka1, va1, ka2, va2, s1, dp1, p2, ds2, stat, rimk, rimt, gsbk, gsbv, grk, grv,
+    termk, termv, wk, wv, gak, gav, hsk, hsv, hrv,
     rsk, rsv, rrk, rrv, pk, pv, g2k, g2v, g3k, g3v,
     rsend, rrecv,
-    tsem, gc_s, gc_r, lsem, ag_s, ag_r, h_s, h_r, b_s, b_r, gg_s, gg_r,
+    g1_s, g1_r, tsem, gc_s, gc_r, lsem, ag_s, ag_r, h_s, h_r, b_s, b_r, gg_s, gg_r,
     hb_s, hb_r, rb_s, rb_r, g2_s, g2_r, g3_s, g3_r, rs_s, rs_r,
 ):
     me = lax.axis_index("seq")
@@ -58,7 +59,6 @@
         locals_.append(pltpu.make_async_copy(k.at[part_of], agk.at[y, i], lsem.at[i]))
         locals_.append(pltpu.make_async_copy(v.at[part_of], agv.at[z, i], lsem.at[ITEMS + i]))
     win_own = [
-        pltpu.make_async_copy(k, wink.at[pl.ds(BLK, 2 * BLK)], lsem.at[2 * ITEMS]),
         pltpu.make_async_copy(v, winv.at[pl.ds(BLK, 2 * BLK)], lsem.at[2 * ITEMS + 1]),
     ]
     list_copies = [
@@ -123,9 +123,7 @@
                 ag_copy(arr, i).start()
 
     halo = [
-        rc(k.at[pl.ds(BLK, BLK)], wink.at[pl.ds(0, BLK)], h_s.at[0], h_r.at[0], right_seq),
         rc(v.at[pl.ds(BLK, BLK)], winv.at[pl.ds(0, BLK)], h_s.at[1], h_r.at[1], right_seq),
-        rc(k.at[pl.ds(0, BLK)], wink.at[pl.ds(3 * BLK, BLK)], h_s.at[2], h_r.at[2], left_seq),
         rc(v.at[pl.ds(0, BLK)], winv.at[pl.ds(3 * BLK, BLK)], h_s.at[3], h_r.at[3], left_seq),
     ]
 
@@ -171,6 +169,22 @@
 
     lax.fori_loop(0, N - 1, eighth, 0)
 
+    key_rims = [
+        (0, rc(agk.at[N - 1, pl.ds(HEADS, HEADS)], rimk.at[0], h_s.at[0], h_r.at[0], dev("z", 1))),
+        (N - 1, rc(agk.at[0, pl.ds(0, HEADS)], rimk.at[1], h_s.at[2], h_r.at[2], dev("z", -1))),
+    ]
+    for end, copy in key_rims:
+        pl.when(y == end)(copy.start)
+
+    @pl.when(y > 0)
+    def _():
+        rimk[0] = agk[(y + N - 1) % N, pl.ds(HEADS, HEADS)]
+
+    @pl.when(y < N - 1)
+    def _():
+        rimk[1] = agk[(y + 1) % N, pl.ds(0, HEADS)]
+
+
     def code_of(s, dest):
         return jnp.maximum(entry_of(s, dest) % 16 - 1, 0)
 
@@ -188,8 +202,8 @@
         rc(sv.at[j], rv.at[y], b_s.at[1, j], b_r.at[1, j], z * N + yd).start()
         return carry
 
-    lax.fori_loop(0, N - 1, bundle, 0)
-    fill(rk.at[z], rv.at[y], z, y)
+    early = 3
+    lax.fori_loop(0, early, bundle, 0)
 
     def eighth_wait(j, carry):
         d = far_first(j)
@@ -223,8 +237,13 @@
     gk[y] = gck[pick(y) // (2 * N)]
     gv[z] = gcv[pick(z) // 2 % N]
     small(gk, gv, gg_s, gg_r, "y", "z")
+    lax.fori_loop(early, N - 1, bundle, 0)
+    fill(rk.at[z], rv.at[y], z, y)
     for c_ in halo:
         c_.wait_recv()
+    for end, copy in key_rims:
+        pl.when(y == end)(copy.wait_recv)
+    small_wait(gk, gv, gg_s, gg_r, "y", "z")
 
     def bundle_wait(j, carry):
         d = far_first(j)
@@ -234,77 +253,81 @@
         rc(sv.at[j], rv.at[ys], b_s.at[1, j], b_r.at[1, j], z * N + ys).wait_recv()
         return carry
 
+    scale = HD ** (-0.5)
+    near = (3 + NGLOB) * BLK
+    rows_by_cols = (((1,), (0,)), ((), ()))
+
+    def dot(lhs, rhs, dims):
+        return lax.dot_general(lhs, rhs, dims, preferred_element_type=F32)
+
+    def over_pairs(one):
+        def head(h, carry):
+            cols = pl.ds(pl.multiple_of(h * HD, HD), HD)
+            for b in range(2):
+                one(h, b, 2 * h + b, pl.ds(b * BLK, BLK), cols)
+            return carry
+
+        lax.fori_loop(0, HEADS, head, 0)
+
+    def first(h, b, i, rows, cols):
+        trio = (rimk[0, h], agk[y, h], agk[y, HEADS + h], rimk[1, h])
+        for j in range(3):
+            ka1[i, pl.ds(j * BLK, BLK)] = trio[b + j]
+        va1[i, pl.ds(0, 3 * BLK)] = winv[pl.ds(b * BLK, 3 * BLK), cols]
+        for buf, glo in ((ka1, gk), (va1, gv)):
+            for gi in range(NGLOB):
+                buf[i, pl.ds((3 + gi) * BLK, BLK)] = glo[gi * HEADS + h]
+        s = dot(q[rows, cols], ka1[i], ROWS_T) * scale
+        key_id = lax.broadcasted_iota(jnp.int32, (BLK, near), 1)
+        if b == 0:
+            bad = (key_id < BLK) & (me == 0)
+        else:
+            bad = (key_id >= 2 * BLK) & (key_id < 3 * BLK) & (me == total - 1)
+        s = jnp.where(bad, -jnp.inf, s)
+        m = jnp.max(s, -1, keepdims=True)
+        e = jnp.exp(s - m)
+        dp = dot(g[rows, cols], va1[i], ROWS_T)
+        s1[i], dp1[i] = e, dp
+        stat[0, i] = m
+        stat[1, i] = jnp.sum(e, -1, keepdims=True)
+        stat[2, i] = jnp.sum(e * dp, -1, keepdims=True)
+
+    over_pairs(first)
     lax.fori_loop(0, N - 1, bundle_wait, 0)
-    small_wait(gk, gv, gg_s, gg_r, "y", "z")
-
-    scale = HD ** (-0.5)
-    key_count = (3 + NRAND + NGLOB) * BLK
-
-    def head(h, carry):
-        cols = pl.ds(pl.multiple_of(h * HD, HD), HD)
+
+    def second(h, b, i, rows, cols):
+        for r in range(NRAND):
+            src = rbs[r, h, 2 * me + b] // 2
+            ka2[i, pl.ds(r * BLK, BLK)] = rk[src // N, src % N]
+            va2[i, pl.ds(r * BLK, BLK)] = rv[src % N, src // N]
+        qb, gb = q[rows, cols], g[rows, cols]
+        far = dot(qb, ka2[i], ROWS_T) * scale
+        dp2 = dot(gb, va2[i], ROWS_T)
+        m1 = stat[0, i]
+        m = jnp.maximum(m1, jnp.max(far, -1, keepdims=True))
+        shrink = jnp.exp(m1 - m)
+        ef = jnp.exp(far - m)
+        inv = 1.0 / (shrink * stat[1, i] + jnp.sum(ef, -1, keepdims=True))
+        delta = (shrink * stat[2, i] + jnp.sum(ef * dp2, -1, keepdims=True)) * inv
+        pf = ef * inv
+        pf_low = pf.astype(BF16)
+        dsf = (scale * pf * (dp2 - delta)).astype(BF16)
+        p2[i], ds2[i] = pf_low, dsf
+        stat[0, i] = shrink * inv
+        stat[1, i] = delta
+        for lhs, rhs, term in ((dsf, qb, termk), (pf_low, gb, termv)):
+            t = dot(lhs, rhs, COLS_T)
+            for r in range(NRAND):
+                term[(h * NRAND + r) * 2 + b] = t[r * BLK : (r + 1) * BLK].astype(BF16)
+
+    for h in range(HEADS):
         for b in range(2):
-            rows = pl.ds(b * BLK, BLK)
-            kb, vb = ka.at[b], va.at[b]
-            kb[pl.ds(0, 3 * BLK)] = wink[pl.ds(b * BLK, 3 * BLK), cols]
-            vb[pl.ds(0, 3 * BLK)] = winv[pl.ds(b * BLK, 3 * BLK), cols]
-            for r in range(NRAND):
-                src = rbs[r, h, 2 * me + b] // 2
-                kb[pl.ds((3 + r) * BLK, BLK)] = rk[src // N, src % N]
-                vb[pl.ds((3 + r) * BLK, BLK)] = rv[src % N, src // N]
-            for gi in range(NGLOB):
-                kb[pl.ds((6 + gi) * BLK, BLK)] = gk[gi * HEADS + h]
-                vb[pl.ds((6 + gi) * BLK, BLK)] = gv[gi * HEADS + h]
-            kall, vall = kb[...], vb[...]
-            qb, gb = q[rows, cols], g[rows, cols]
-            s = lax.dot_general(qb, kall, ROWS_T, preferred_element_type=F32) * scale
-            key_id = lax.broadcasted_iota(jnp.int32, (BLK, key_count), 1)
-            if b == 0:
-                bad = (key_id < BLK) & (me == 0)
-            else:
-                bad = (key_id >= 2 * BLK) & (key_id < 3 * BLK) & (me == total - 1)
-            s = jnp.where(bad, -jnp.inf, s)
-            m = jnp.max(s, -1, keepdims=True)
-            e = jnp.exp(s - m)
-            p = e * (1.0 / jnp.sum(e, -1, keepdims=True))
-            plow = p.astype(BF16)
-            o = lax.dot_general(plow, vall, (((1,), (0,)), ((), ())), preferred_element_type=F32).astype(BF16)
-            delta = jnp.sum(gb.astype(F32) * o.astype(F32), -1, keepdims=True)
-            dp = lax.dot_general(gb, vall, ROWS_T, preferred_element_type=F32)
-            ds = (scale * p * (dp - delta)).astype(BF16)
-            att[rows, cols] = o
-            dq[rows, cols] = lax.dot_general(
-                ds, kall, (((1,), (0,)), ((), ())), preferred_element_type=F32
-            ).astype(BF16)
-            for lhs, rhs, win, term, gacc in ((ds, qb, wk, termk, gak), (plow, gb, wv, termv, gav)):
-                t = lax.dot_general(lhs, rhs, COLS_T, preferred_element_type=F32)
-                if b == 0:
-                    win[pl.ds(0, 3 * BLK), cols] = t[: 3 * BLK]
-                else:
-                    win[pl.ds(BLK, 2 * BLK), cols] += t[: 2 * BLK]
-                    win[pl.ds(3 * BLK, BLK), cols] = t[2 * BLK : 3 * BLK]
-                for r in range(NRAND):
-                    term[(h * NRAND + r) * 2 + b] = t[(3 + r) * BLK : (4 + r) * BLK].astype(BF16)
-                for gi in range(NGLOB):
-                    piece = t[(6 + gi) * BLK : (7 + gi) * BLK]
-                    if b == 0:
-                        gacc[gi * HEADS + h] = piece
-                    else:
-                        gacc[gi * HEADS + h] += piece
-        return carry
-
-    lax.fori_loop(0, HEADS, head, 0)
+            second(h, b, 2 * h + b, pl.ds(b * BLK, BLK), pl.ds(h * HD, HD))
 
     def fill_back(dst_k, dst_v, zd, yd):
         for s in range(N):
             dst_k[s] = termk[entry_of(zd * N + s, me) // 16]
             dst_v[s] = termv[entry_of(s * N + yd, me) // 16]
-        dst_k[N] = gak[zd].astype(BF16)
-        dst_v[N] = gav[yd].astype(BF16)
-
-    hsk[0] = wk[pl.ds(0, BLK)].astype(BF16)
-    hsk[1] = wk[pl.ds(3 * BLK, BLK)].astype(BF16)
-    hsv[0] = wv[pl.ds(0, BLK)].astype(BF16)
-    hsv[1] = wv[pl.ds(3 * BLK, BLK)].astype(BF16)
 
     def back(j, carry):
         d = far_first(j)
@@ -317,12 +340,66 @@
 
     lax.fori_loop(0, N - 1, back, 0)
     fill_back(rrk.at[z], rrv.at[y], z, y)
+
+    def third(h, b, i, rows, cols):
+        qb, gb = q[rows, cols], g[rows, cols]
+        pn = s1[i] * stat[0, i]
+        pn_low = pn.astype(BF16)
+        dsn = (scale * pn * (dp1[i] - stat[1, i])).astype(BF16)
+        att[rows, cols] = (dot(pn_low, va1[i], rows_by_cols) + dot(p2[i], va2[i], rows_by_cols)).astype(BF16)
+        dq[rows, cols] = (dot(dsn, ka1[i], rows_by_cols) + dot(ds2[i], ka2[i], rows_by_cols)).astype(BF16)
+        for lhs, rhs, win, gacc in ((dsn, qb, wk, gak), (pn_low, gb, wv, gav)):
+            t = dot(lhs, rhs, COLS_T)
+            if b == 0:
+                win[pl.ds(0, 3 * BLK), cols] = t[: 3 * BLK]
+            else:
+                win[pl.ds(BLK, 2 * BLK), cols] += t[: 2 * BLK]
+                win[pl.ds(3 * BLK, BLK), cols] = t[2 * BLK : 3 * BLK]
+            for gi in range(NGLOB):
+                piece = t[(3 + gi) * BLK : (4 + gi) * BLK]
+                if b == 0:
+                    gacc[gi * HEADS + h] = piece
+                else:
+                    gacc[gi * HEADS + h] += piece
+
+    over_pairs(third)
+    for h in range(HEADS):
+        hsk[0, h] = wk[pl.ds(0, BLK), pl.ds(h * HD, HD)].astype(BF16)
+        hsk[1, h] = wk[pl.ds(3 * BLK, BLK), pl.ds(h * HD, HD)].astype(BF16)
+    hsv[0] = wv[pl.ds(0, BLK)].astype(BF16)
+    hsv[1] = wv[pl.ds(3 * BLK, BLK)].astype(BF16)
+    gsbk[...] = gak[...].astype(BF16)
+    gsbv[...] = gav[...].astype(BF16)
+    grk[z] = gak[z].astype(BF16)
+    grv[y] = gav[y].astype(BF16)
+
+    def glob_back(j, carry):
+        d = far_first(j)
+        zd = (z + d) % N
+        yd = (y + d) % N
+        rc(gsbk.at[zd], grk.at[z], g1_s.at[0, j], g1_r.at[0, j], zd * N + y).start()
+        rc(gsbv.at[yd], grv.at[y], g1_s.at[1, j], g1_r.at[1, j], z * N + yd).start()
+        return carry
+
+    def glob_back_wait(j, carry):
+        d = far_first(j)
+        zs = (z + N - d) % N
+        ys = (y + N - d) % N
+        rc(gsbk.at[zs], grk.at[zs], g1_s.at[0, j], g1_r.at[0, j], zs * N + y).wait_recv()
+        rc(gsbv.at[ys], grv.at[ys], g1_s.at[1, j], g1_r.at[1, j], z * N + ys).wait_recv()
+        return carry
+
+    lax.fori_loop(0, N - 1, glob_back, 0)
     halo_back = [
-        rc(hsk.at[0], hrk.at[1], hb_s.at[0], hb_r.at[0], left_seq),
-        rc(hsk.at[1], hrk.at[0], hb_s.at[1], hb_r.at[1], right_seq),
         rc(hsv.at[0], hrv.at[1], hb_s.at[2], hb_r.at[2], left_seq),
         rc(hsv.at[1], hrv.at[0], hb_s.at[3], hb_r.at[3], right_seq),
     ]
+    rim_back = [
+        (0, rc(hsk.at[0], rimt.at[0], hb_s.at[0], hb_r.at[0], dev("z", -1))),
+        (N - 1, rc(hsk.at[1], rimt.at[1], hb_s.at[1], hb_r.at[1], dev("z", 1))),
+    ]
+    for end, copy in rim_back:
+        pl.when(y == end)(copy.start)
     for c_ in halo_back:
         c_.start()
 
@@ -334,44 +411,74 @@
         rc(rsv.at[j], rrv.at[ys], rb_s.at[1, j], rb_r.at[1, j], z * N + ys).wait_recv()
         return carry
 
-    lax.fori_loop(0, N - 1, back_wait, 0)
+    tile = 16
+    arrivals = [(0, 4, 3, 5), (2, 6), (1, 7)]
+
+    def partial(rel, wave):
+        for buf, part, p in ((rrk, pk, y), (rrv, pv, z)):
+            tgt = (p + rel) % N
+            weight, rows_of = [], []
+            for d in arrivals[wave]:
+                if buf is rrk:
+                    s = (z + N - d) % N
+                    code = entry_of(z * N + tgt, s * N + y) % 16
+                else:
+                    s = (y + N - d) % N
+                    code = entry_of(tgt * N + y, z * N + s) % 16
+                rows_of.append(s)
+                weight.append([jnp.where(code == i + 1, 1.0, 0.0).astype(F32) for i in range(ITEMS)])
+
+            def rows_step(i, carry, buf=buf, part=part, tgt=tgt, weight=weight, rows_of=rows_of):
+                rows = pl.ds(pl.multiple_of(i * tile, tile), tile)
+                acc = [None if wave == 0 else part[tgt, c, rows] for c in range(ITEMS)]
+                for s, ws in zip(rows_of, weight):
+                    x = buf[s, tgt, rows].astype(F32)
+                    for c in range(ITEMS):
+                        w = x * ws[c]
+                        acc[c] = w if acc[c] is None else acc[c] + w
+                for c in range(ITEMS):
+                    part[tgt, c, rows] = acc[c]
+                return carry
+
+            lax.fori_loop(0, BLK // tile, rows_step, 0)
+
+    def step_loop(first_rel, stride, count, wave=2):
+        def more(j, carry):
+            partial((first_rel + stride * j) % N, wave)
+            return carry
+
+        lax.fori_loop(0, count, more, 0)
+
+    lax.fori_loop(0, 3, back_wait, 0)
+    step_loop(0, 1, N, 0)
+    lax.fori_loop(3, 5, back_wait, 0)
+    step_loop(0, 1, N, 1)
+    for end, copy in rim_back:
+        pl.when(y == end)(copy.wait_recv)
+
+    @pl.when(y > 0)
+    def _():
+        pk[(y + N - 1) % N, pl.ds(HEADS, HEADS)] += hsk[0].astype(F32)
+
+    @pl.when(y == 0)
+    def _():
+        pk[N - 1, pl.ds(HEADS, HEADS)] += rimt[0].astype(F32)
+
+    @pl.when(y < N - 1)
+    def _():
+        pk[(y + 1) % N, pl.ds(0, HEADS)] += hsk[1].astype(F32)
+
+    @pl.when(y == N - 1)
+    def _():
+        pk[0, pl.ds(0, HEADS)] += rimt[1].astype(F32)
+
+    lax.fori_loop(5, N - 1, back_wait, 0)
 
     def total_of(read):
         acc = read(0).astype(F32)
         for s in range(1, N):
             acc += read(s).astype(F32)
         return acc.astype(BF16)
-
-    g2k[y] = total_of(lambda s: rrk[s, N])
-    g2v[z] = total_of(lambda s: rrv[s, N])
-    small(g2k, g2v, g2_s, g2_r, "y", "z")
-
-    tile = 16
-
-    def partial(rel):
-        for buf, part, p in ((rrk, pk, y), (rrv, pv, z)):
-            tgt = (p + rel) % N
-            weight = []
-            for s in range(N):
-                if buf is rrk:
-                    code = entry_of(z * N + tgt, s * N + y) % 16
-                else:
-                    code = entry_of(tgt * N + y, z * N + s) % 16
-                weight.append([jnp.where(code == i + 1, 1.0, 0.0).astype(F32) for i in range(ITEMS)])
-
-            def rows_step(i, carry, buf=buf, part=part, tgt=tgt, weight=weight):
-                rows = pl.ds(pl.multiple_of(i * tile, tile), tile)
-                acc = [None] * ITEMS
-                for s in range(N):
-                    x = buf[s, tgt, rows].astype(F32)
-                    for c in range(ITEMS):
-                        w = x * weight[s][c]
-                        acc[c] = w if acc[c] is None else acc[c] + w
-                for c in range(ITEMS):
-                    part[tgt, c, rows] = acc[c]
-                return carry
-
-            lax.fori_loop(0, BLK // tile, rows_step, 0)
 
     rs_index = {key: i for i, key in enumerate(RS)}
 
@@ -393,25 +500,21 @@
             rsend[arr, i] = x.astype(BF16)
             rs_copy(arr, i).start()
 
-    def step_loop(first, stride, count):
-        def body(j, carry):
-            partial(first + stride * j)
-            return carry
-
-        lax.fori_loop(0, count, body, 0)
-
     step_loop(3, 1, 3)
     for f in range(4):
         rs_send(f, 1)
     step_loop(2, 4, 2)
+    lax.fori_loop(0, N - 1, glob_back_wait, 0)
+    g2k[y] = total_of(lambda s: grk[s])
+    g2v[z] = total_of(lambda s: grv[s])
+    small(g2k, g2v, g2_s, g2_r, "y", "z")
     for f in range(4):
         rs_send(f, 2)
+    step_loop(7, 1, 3)
     small_wait(g2k, g2v, g2_s, g2_r, "y", "z")
     g3k[z] = total_of(lambda s: g2k[s])
     g3v[y] = total_of(lambda s: g2v[s])
     small(g3k, g3v, g3_s, g3_r, "z", "y")
-    step_loop(0, 1, 2)
-    step_loop(7, 1, 1)
     for f in range(4):
         rs_send(f, 3)
     for f in range(2):
@@ -420,25 +523,29 @@
         c_.wait_recv()
     small_wait(g3k, g3v, g3_s, g3_r, "z", "y")
 
-    for f in (2, 3, 0, 1):
-        for arr in (0, 1):
-            rs_copy(arr, rs_index[(f, FLOWS[f][2])]).wait_recv()
-    for arr, part, p, win, hr, g3, out in (
-        (0, pk, y, wk, hrk, g3k, dk),
-        (1, pv, z, wv, hrv, g3v, dv),
-    ):
+    parts = ((0, pk, y, wk, None, g3k, dk), (1, pv, z, wv, hrv, g3v, dv))
+    for arr, part, p, win, hr, g3, out in parts:
         for b in range(2):
-            flows = [f for f in range(4) if FLOWS[f][1] == b]
+            mine = [jnp.where(gblk[gi] == me * 2 + b, 1.0, 0.0).astype(F32) for gi in range(NGLOB)]
             for h in range(HEADS):
                 cols = pl.ds(h * HD, HD)
-                x = win[pl.ds((1 + b) * BLK, BLK), cols] + hr[b, :, cols].astype(F32)
-                x += part[p, b * HEADS + h]
-                for f in flows:
-                    x += rrecv[arr, rs_index[(f, FLOWS[f][2])], h].astype(F32)
+                x = part[p, b * HEADS + h] + win[pl.ds((1 + b) * BLK, BLK), cols]
+                if hr is not None:
+                    x += hr[b, :, cols].astype(F32)
                 for gi in range(NGLOB):
-                    mine = jnp.where(gblk[gi] == me * 2 + b, 1.0, 0.0).astype(F32)
-                    x += g3[gi * HEADS + h].astype(F32) * mine
-                out[pl.ds(b * BLK, BLK), cols] = x.astype(BF16)
+                    x += g3[gi * HEADS + h].astype(F32) * mine[gi]
+                part[p, b * HEADS + h] = x
+    for f in (2, 3, 0, 1):
+        i = rs_index[(f, FLOWS[f][2])]
+        b = FLOWS[f][1]
+        for arr, part, p, win, hr, g3, out in parts:
+            rs_copy(arr, i).wait_recv()
+            for h in range(HEADS):
+                x = part[p, b * HEADS + h] + rrecv[arr, i, h].astype(F32)
+                if f < 2:
+                    out[pl.ds(b * BLK, BLK), pl.ds(h * HD, HD)] = x.astype(BF16)
+                else:
+                    part[p, b * HEADS + h] = x
 
     for arr in (0, 1):
         for i in range(len(AG)):
@@ -447,6 +554,8 @@
             rs_copy(arr, i).wait_send()
     for c_ in halo + halo_back:
         c_.wait_send()
+    for end, copy in key_rims + rim_back:
+        pl.when(y == end)(copy.wait_send)
 
     def drain(j, carry):
         for a, (bk, bv) in ((b_s, (sk, sv)), (rb_s, (rsk, rsv))):
@@ -459,6 +568,8 @@
         ):
             rc(bk.at[ik], bk.at[ik], a.at[0, j], gg_r.at[0, j], me).wait_send()
             rc(bv.at[iv], bv.at[iv], a.at[1, j], gg_r.at[1, j], me).wait_send()
+        rc(gsbk.at[z], grk.at[z], g1_s.at[0, j], g1_r.at[0, j], me).wait_send()
+        rc(gsbv.at[y], grv.at[y], g1_s.at[1, j], g1_r.at[1, j], me).wait_send()
         rc(gsk, gck.at[z], gc_s.at[0, j], gc_r.at[0, j], me).wait_send()
         rc(gsv, gcv.at[y], gc_s.at[1, j], gc_r.at[1, j], me).wait_send()
         return carry
@@ -476,7 +587,7 @@
     full = jax.ShapeDtypeStruct(queries.shape, BF16)
     vm, dma = pltpu.VMEM, pltpu.SemaphoreType.DMA
     bund = lambda n, slots: vm((n, slots, BLK, HD), BF16)
-    keys_n = (3 + NRAND + NGLOB) * BLK
+    near, far = (3 + NGLOB) * BLK, NRAND * BLK
     small = vm((N, BLK, HD), BF16)
     scratch = [
         vm(queries.shape, BF16), vm(queries.shape, BF16),
@@ -484,20 +595,26 @@
         vm((N * N, 2 * N * N), jnp.int32), pltpu.SMEM((N * N, 2 * N * N), jnp.int32),
         vm((BLK, HD), BF16), vm((BLK, HD), BF16), small, small,
         vm((N, ITEMS, BLK, HD), BF16), vm((N, ITEMS, BLK, HD), BF16),
-        vm((4 * BLK, HEADS * HD), BF16), vm((4 * BLK, HEADS * HD), BF16),
+        vm((4 * BLK, HEADS * HD), BF16),
         bund(N - 1, N), bund(N - 1, N), bund(N, N), bund(N, N),
         vm((N, BLK, HD), BF16), vm((N, BLK, HD), BF16),
-        vm((2, keys_n, HD), BF16), vm((2, keys_n, HD), BF16),
+        vm((ITEMS, near, HD), BF16), vm((ITEMS, near, HD), BF16),
+        vm((ITEMS, far, HD), BF16), vm((ITEMS, far, HD), BF16),
+        vm((ITEMS, BLK, near), F32), vm((ITEMS, BLK, near), F32),
+        vm((ITEMS, BLK, far), BF16), vm((ITEMS, BLK, far), BF16),
+        vm((3, ITEMS, BLK, 1), F32), vm((2, HEADS, BLK, HD), BF16), vm((2, HEADS, BLK, HD), BF16),
+        small, small, small, small,
         vm((24, BLK, HD), BF16), vm((24, BLK, HD), BF16),
         vm((4 * BLK, HEADS * HD), F32), vm((4 * BLK, HEADS * HD), F32),
         vm((N, BLK, HD), F32), vm((N, BLK, HD), F32),
-        vm((2, BLK, HEADS * HD), BF16), vm((2, BLK, HEADS * HD), BF16),
-        vm((2, BLK, HEADS * HD), BF16), vm((2, BLK, HEADS * HD), BF16),
-        bund(N - 1, N + 1), bund(N - 1, N + 1), bund(N, N + 1), bund(N, N + 1),
+        vm((2, HEADS, BLK, HD), BF16), vm((2, BLK, HEADS * HD), BF16),
+        vm((2, BLK, HEADS * HD), BF16),
+        bund(N - 1, N), bund(N - 1, N), bund(N, N), bund(N, N),
         vm((N, ITEMS, BLK, HD), F32), vm((N, ITEMS, BLK, HD), F32),
         vm((N, BLK, HD), BF16), vm((N, BLK, HD), BF16),
         vm((N, BLK, HD), BF16), vm((N, BLK, HD), BF16),
         vm((2, len(RS), HEADS, BLK, HD), BF16), vm((2, len(RS), HEADS, BLK, HD), BF16),
+        dma((2, N - 1)), dma((2, N - 1)),
         dma, dma((2, N - 1)), dma((2, N - 1)), dma((2 * ITEMS + 6,)), dma((2, len(AG))), dma((2, len(AG))), dma((4,)), dma((4,)),
         dma((2, N - 1)), dma((2, N - 1)), dma((2, N - 1)), dma((2, N - 1)),
         dma((4,)), dma((4,)), dma((2, N - 1)), dma((2, N - 1)),

time: 130 us -> 125 us (0.962)
  Pallas kernels: 129 us -> 124 us
    pallas_call x1, Pallas kernels: 127 us -> 122 us  [body(): pl.pallas_call(kernel, out_shape=(full,) * 4, in_specs=[smem] + [pl.Block...]
where the time goes in v3:
time: 125 us
  Pallas kernels  124 us (99%)
    pallas_call x1, Pallas kernels, body(): pl.pallas_call(kernel, out_shape=(full,) * 4, in_specs=[smem] + [pl.Block...  122 us

profile of v3, /device:TPU:14, one launch (start us, length us, event | category | flops | bytes accessed | tf_op | source)
XLA Modules:
  0.0 124.9 jit_solution(15099607285538537712)
XLA Ops:
  0.6 122.3 %shard_map.93 = (bf16[128,512]{1,0:T(8,128)(2,1)}, bf16[128,512]{1,0:T(8,128)(2,1)}, bf16[128,512]{1,0:T(8,128)(2,1)}, bf16[128,512]{1,0:T(8,128)(2,1)}) custom-call(s32[2]{0:T(128)} %glb.1, s32[3,4,128]{2,1,0:T(4,128)} %bitcast.1, bf16[128,512]{1,0:T(8,128)(2,1)} %q_hbm.1, bf16[128,512]{1,0:T(8,128)(2,1)} %k.1, bf16[128,512]{1,0:T(8,128)(2,1)} %v.1, ...), custom_call_target="tpu_custom_call" | custom-call | tf_op jit(solution)/shard_map/pallas_call | solution.py:626
  123.0 1.9 %shard_map.94 = (bf16[128,512]{1,0:T(8,128)(2,1)}, bf16[128,512]{1,0:T(8,128)(2,1)}, bf16[128,512]{1,0:T(8,128)(2,1)}, bf16[128,512]{1,0:T(8,128)(2,1)}) custom-call(bf16[128,512]{1,0:T(8,128)(2,1)} %get-tuple-element.8.refs_0_, bf16[128,512]{1,0:T(8,128)(2,1)} %get-tuple-element.9.refs_1_, bf16[128,512]{1,0:T(8,128)(2,1)} %get-tuple-element.10.refs_2_, ...), custom_call_target="tpu_custom_call" | custom-call | tf_op jit(solution)/shard_map/pallas_call | solution.py:634

commit v4 on v3

--- a/solution.py
+++ b/solution.py
@@ -504,19 +504,19 @@
     for f in range(4):
         rs_send(f, 1)
     step_loop(2, 4, 2)
+    for f in range(4):
+        rs_send(f, 2)
     lax.fori_loop(0, N - 1, glob_back_wait, 0)
     g2k[y] = total_of(lambda s: grk[s])
     g2v[z] = total_of(lambda s: grv[s])
     small(g2k, g2v, g2_s, g2_r, "y", "z")
+    step_loop(7, 1, 3)
     for f in range(4):
-        rs_send(f, 2)
-    step_loop(7, 1, 3)
+        rs_send(f, 3)
     small_wait(g2k, g2v, g2_s, g2_r, "y", "z")
     g3k[z] = total_of(lambda s: g2k[s])
     g3v[y] = total_of(lambda s: g2v[s])
     small(g3k, g3v, g3_s, g3_r, "z", "y")
-    for f in range(4):
-        rs_send(f, 3)
     for f in range(2):
         rs_send(f, 4)
     for c_ in halo_back:

time: 125 us -> 128 us (1.024)
  Pallas kernels: 124 us -> 128 us
    pallas_call x1, Pallas kernels: 122 us -> 126 us  [body(): pl.pallas_call(kernel, out_shape=(full,) * 4, in_specs=[smem] + [pl.Block...]
where the time goes in v4:
time: 128 us
  Pallas kernels  128 us (100%)
    pallas_call x1, Pallas kernels, body(): pl.pallas_call(kernel, out_shape=(full,) * 4, in_specs=[smem] + [pl.Block...  126 us

profile of v4, /device:TPU:14, one launch (start us, length us, event | category | flops | bytes accessed | tf_op | source)
XLA Modules:
  0.0 128.3 jit_solution(5563815790117088542)
XLA Ops:
  0.6 125.7 %shard_map.93 = (bf16[128,512]{1,0:T(8,128)(2,1)}, bf16[128,512]{1,0:T(8,128)(2,1)}, bf16[128,512]{1,0:T(8,128)(2,1)}, bf16[128,512]{1,0:T(8,128)(2,1)}) custom-call(s32[2]{0:T(128)} %glb.1, s32[3,4,128]{2,1,0:T(4,128)} %bitcast.1, bf16[128,512]{1,0:T(8,128)(2,1)} %q_hbm.1, bf16[128,512]{1,0:T(8,128)(2,1)} %k.1, bf16[128,512]{1,0:T(8,128)(2,1)} %v.1, ...), custom_call_target="tpu_custom_call" | custom-call | tf_op jit(solution)/shard_map/pallas_call | solution.py:626
  126.4 1.9 %shard_map.94 = (bf16[128,512]{1,0:T(8,128)(2,1)}, bf16[128,512]{1,0:T(8,128)(2,1)}, bf16[128,512]{1,0:T(8,128)(2,1)}, bf16[128,512]{1,0:T(8,128)(2,1)}) custom-call(bf16[128,512]{1,0:T(8,128)(2,1)} %get-tuple-element.8.refs_0_, bf16[128,512]{1,0:T(8,128)(2,1)} %get-tuple-element.9.refs_1_, bf16[128,512]{1,0:T(8,128)(2,1)} %get-tuple-element.10.refs_2_, ...), custom_call_target="tpu_custom_call" | custom-call | tf_op jit(solution)/shard_map/pallas_call | solution.py:634

commit v5 on v3

--- a/solution.py
+++ b/solution.py
@@ -338,7 +338,7 @@
         rc(rsv.at[j], rrv.at[y], rb_s.at[1, j], rb_r.at[1, j], z * N + yd).start()
         return carry
 
-    lax.fori_loop(0, N - 1, back, 0)
+    lax.fori_loop(0, N - 3, back, 0)
     fill_back(rrk.at[z], rrv.at[y], z, y)
 
     def third(h, b, i, rows, cols):
@@ -390,6 +390,7 @@
         return carry
 
     lax.fori_loop(0, N - 1, glob_back, 0)
+    lax.fori_loop(N - 3, N - 1, back, 0)
     halo_back = [
         rc(hsv.at[0], hrv.at[1], hb_s.at[2], hb_r.at[2], left_seq),
         rc(hsv.at[1], hrv.at[0], hb_s.at[3], hb_r.at[3], right_seq),
@@ -449,36 +450,40 @@
 
         lax.fori_loop(0, count, more, 0)
 
-    lax.fori_loop(0, 3, back_wait, 0)
-    step_loop(0, 1, N, 0)
-    lax.fori_loop(3, 5, back_wait, 0)
-    step_loop(0, 1, N, 1)
-    for end, copy in rim_back:
-        pl.when(y == end)(copy.wait_recv)
-
-    @pl.when(y > 0)
-    def _():
-        pk[(y + N - 1) % N, pl.ds(HEADS, HEADS)] += hsk[0].astype(F32)
-
-    @pl.when(y == 0)
-    def _():
-        pk[N - 1, pl.ds(HEADS, HEADS)] += rimt[0].astype(F32)
-
-    @pl.when(y < N - 1)
-    def _():
-        pk[(y + 1) % N, pl.ds(0, HEADS)] += hsk[1].astype(F32)
-
-    @pl.when(y == N - 1)
-    def _():
-        pk[0, pl.ds(0, HEADS)] += rimt[1].astype(F32)
-
-    lax.fori_loop(5, N - 1, back_wait, 0)
-
     def total_of(read):
         acc = read(0).astype(F32)
         for s in range(1, N):
             acc += read(s).astype(F32)
         return acc.astype(BF16)
+
+    lax.fori_loop(0, 3, back_wait, 0)
+    step_loop(0, 1, N, 0)
+    lax.fori_loop(3, 5, back_wait, 0)
+    step_loop(0, 1, N, 1)
+    lax.fori_loop(0, N - 1, glob_back_wait, 0)
+    g2k[y] = total_of(lambda s: grk[s])
+    g2v[z] = total_of(lambda s: grv[s])
+    small(g2k, g2v, g2_s, g2_r, "y", "z")
+    for end, copy in rim_back:
+        pl.when(y == end)(copy.wait_recv)
+
+    @pl.when(y > 0)
+    def _():
+        pk[(y + N - 1) % N, pl.ds(HEADS, HEADS)] += hsk[0].astype(F32)
+
+    @pl.when(y == 0)
+    def _():
+        pk[N - 1, pl.ds(HEADS, HEADS)] += rimt[0].astype(F32)
+
+    @pl.when(y < N - 1)
+    def _():
+        pk[(y + 1) % N, pl.ds(0, HEADS)] += hsk[1].astype(F32)
+
+    @pl.when(y == N - 1)
+    def _():
+        pk[0, pl.ds(0, HEADS)] += rimt[1].astype(F32)
+
+    lax.fori_loop(5, N - 1, back_wait, 0)
 
     rs_index = {key: i for i, key in enumerate(RS)}
 
@@ -504,17 +509,13 @@
     for f in range(4):
         rs_send(f, 1)
     step_loop(2, 4, 2)
-    lax.fori_loop(0, N - 1, glob_back_wait, 0)
-    g2k[y] = total_of(lambda s: grk[s])
-    g2v[z] = total_of(lambda s: grv[s])
-    small(g2k, g2v, g2_s, g2_r, "y", "z")
-    for f in range(4):
-        rs_send(f, 2)
-    step_loop(7, 1, 3)
     small_wait(g2k, g2v, g2_s, g2_r, "y", "z")
     g3k[z] = total_of(lambda s: g2k[s])
     g3v[y] = total_of(lambda s: g2v[s])
     small(g3k, g3v, g3_s, g3_r, "z", "y")
+    for f in range(4):
+        rs_send(f, 2)
+    step_loop(7, 1, 3)
     for f in range(4):
         rs_send(f, 3)
     for f in range(2):

time: 125 us -> 125 us (level)
  no operation moved by 1% of the time
where the time goes in v5:
time: 125 us
  Pallas kernels  124 us (99%)
    pallas_call x1, Pallas kernels, body(): pl.pallas_call(kernel, out_shape=(full,) * 4, in_specs=[smem] + [pl.Block...  122 us

profile of v5, /device:TPU:14, one launch (start us, length us, event | category | flops | bytes accessed | tf_op | source)
XLA Modules:
  0.0 124.5 jit_solution(5660805377086694381)
XLA Ops:
  0.6 122.0 %shard_map.93 = (bf16[128,512]{1,0:T(8,128)(2,1)}, bf16[128,512]{1,0:T(8,128)(2,1)}, bf16[128,512]{1,0:T(8,128)(2,1)}, bf16[128,512]{1,0:T(8,128)(2,1)}) custom-call(s32[2]{0:T(128)} %glb.1, s32[3,4,128]{2,1,0:T(4,128)} %bitcast.1, bf16[128,512]{1,0:T(8,128)(2,1)} %q_hbm.1, bf16[128,512]{1,0:T(8,128)(2,1)} %k.1, bf16[128,512]{1,0:T(8,128)(2,1)} %v.1, ...), custom_call_target="tpu_custom_call" | custom-call | tf_op jit(solution)/shard_map/pallas_call | solution.py:627
  122.6 1.9 %shard_map.94 = (bf16[128,512]{1,0:T(8,128)(2,1)}, bf16[128,512]{1,0:T(8,128)(2,1)}, bf16[128,512]{1,0:T(8,128)(2,1)}, bf16[128,512]{1,0:T(8,128)(2,1)}) custom-call(bf16[128,512]{1,0:T(8,128)(2,1)} %get-tuple-element.8.refs_0_, bf16[128,512]{1,0:T(8,128)(2,1)} %get-tuple-element.9.refs_1_, bf16[128,512]{1,0:T(8,128)(2,1)} %get-tuple-element.10.refs_2_, ...), custom_call_target="tpu_custom_call" | custom-call | tf_op jit(solution)/shard_map/pallas_call | solution.py:635
